TPU v7x, 32 devices: a whole 2x2x4 slice. The times are simulated.
32 devices in a mesh: req: 8 (over z, x), kv: 4 (over y, core).
Axes of the slice: x: 2, y: 2, z: 4, core: 2. Of those that a mesh axis runs over, the one named last changes fastest.
Arguments:
- activations: bfloat16 [1024, 8192], P('kv', 'req'), may hold values from -210 to 210
- input_gain: bfloat16 [8192], P('req'), may hold values from 0.25 to 1.75
- qkv_weight: bfloat16 [8192, 8, 1280], P('req', 'kv'), may hold values from -0.0625 to 0.0625
- out_weight: bfloat16 [8, 1024, 8192], P('kv', None, 'req'), may hold values from -0.1875 to 0.1875
- post_gain: bfloat16 [8192], P('req'), may hold values from 0.25 to 1.75
- cache_entries: bfloat16 [40, 4096, 8, 256], P('req', None, 'kv'), may hold values from -140 to 140
- new_lengths: int32 [8, 5], replicated, may hold values from 1 to 96, 128 in all within a row
- cache_lengths: int32 [8, 5], replicated, may hold values from 1 to 4096, as said below
- request_slot: int32 [40], replicated, may hold values from 0 to 39, each once
Outputs:
- projected: bfloat16 [1024, 8192], P('kv', 'req')
- normed: bfloat16 [1024, 8192], P('kv', 'req')
- appended: bfloat16 [1024, 8, 256], P('req', 'kv')
Inputs may be any that keep to these rules, and one draw needn't show every extreme that they name: `new_lengths`: the 5 requests of one block bring 128 new tokens together; in every block one request brings exactly 96. `cache_lengths`: A request's cache holds fewer than 256 positions or exactly 4096; some request holds 4096. Each number once; request q of the arrival order sits in block request_slot[q] // 5, slot request_slot[q] % 5.
All inputs are finite; a program needn't handle non-finite values.
Results may differ from a plain program's by a relative error of at most 0.012.
The roundings to bfloat16 on the way count: a program that leaves them out, or rounds other values in their place, can miss the bound.
Values may be sent and summed in bfloat16 or wider, within the bound.
A program may use at most 512 MiB of HBM per device.

v0:
```python
import math

import jax
import jax.numpy as jnp
from jax import lax
from jax.sharding import PartitionSpec as P

epsilon_norm = 1e-05
rope_base = 500000.0


def layout(new_lengths, cache_lengths, request_slot, block_tokens):
    blocks, per_block = new_lengths.shape
    request_total = blocks * per_block
    token_total = blocks * block_tokens
    slot_ids = jnp.arange(request_total, dtype=jnp.int32)
    new_flat = new_lengths.reshape(request_total)
    cache_flat = cache_lengths.reshape(request_total)
    chosen = (request_slot[:, None] == slot_ids[None, :]).astype(jnp.int32)
    arrival_len = jnp.sum(chosen * new_flat[None, :], axis=1)
    arrival_start = jnp.cumsum(arrival_len) - arrival_len
    inside = jnp.cumsum(new_lengths, axis=1) - new_lengths
    slot_start = (inside + block_tokens * jnp.arange(blocks, dtype=jnp.int32)[:, None]).reshape(
        request_total
    )
    slot_arrival_start = jnp.sum(chosen * arrival_start[:, None], axis=0)
    positions = jnp.arange(token_total, dtype=jnp.int32)
    slot_of_row = jnp.sum((slot_start[None, :] <= positions[:, None]).astype(jnp.int32), axis=1) - 1
    row_pick = (slot_of_row[:, None] == slot_ids[None, :]).astype(jnp.int32)
    offset_row = positions - jnp.sum(row_pick * slot_start[None, :], axis=1)
    token_of_row = jnp.sum(row_pick * slot_arrival_start[None, :], axis=1) + offset_row
    pos_of_row = jnp.sum(row_pick * cache_flat[None, :], axis=1) + offset_row
    arrival_of_token = (
        jnp.sum((arrival_start[None, :] <= positions[:, None]).astype(jnp.int32), axis=1) - 1
    )
    token_pick = (arrival_of_token[:, None] == slot_ids[None, :]).astype(jnp.int32)
    slot_of_token = jnp.sum(token_pick * request_slot[None, :], axis=1)
    offset_token = positions - jnp.sum(token_pick * arrival_start[None, :], axis=1)
    token_slot_pick = (slot_of_token[:, None] == slot_ids[None, :]).astype(jnp.int32)
    row_of_token = jnp.sum(token_slot_pick * slot_start[None, :], axis=1) + offset_token
    pos_of_token = jnp.sum(token_slot_pick * cache_flat[None, :], axis=1) + offset_token
    return (token_of_row, row_of_token, pos_of_row, pos_of_token, slot_of_row, offset_row)


def rotate(partial_sums, positions, group_size, head_size):
    half_size = head_size // 2
    frequency = jnp.exp(
        -(jnp.arange(half_size, dtype=jnp.float32) * (2.0 / head_size)) * math.log(rope_base)
    )
    angles = positions.astype(jnp.float32)[:, None] * frequency[None, :]
    cosine = jnp.cos(angles)[:, None, None, :]
    sine_part = jnp.sin(angles)[:, None, None, :]
    turned = partial_sums[:, :, : group_size + 1, :]
    first_half = turned[..., :half_size]
    second_half = turned[..., half_size:]
    turned = jnp.concatenate(
        [
            first_half * cosine - second_half * sine_part,
            second_half * cosine + first_half * sine_part,
        ],
        axis=-1,
    )
    return jnp.concatenate([turned, partial_sums[:, :, group_size + 1 :, :]], axis=2)


def slot_attention(
    queries, new_keys, new_values, stored, cached_count, new_count, block_count, key_block
):
    head_size = new_keys.shape[-1]
    score_scale = 1.0 / math.sqrt(head_size)
    row_count = queries.shape[0]
    heads_here = queries.shape[1]
    group_size = queries.shape[2]
    slot_length = stored.shape[0]
    offsets = jnp.arange(row_count, dtype=jnp.int32)
    new_valid = (offsets[None, :] <= offsets[:, None]) & (offsets[None, :] < new_count)
    new_scores = (
        jnp.einsum("ihgd,jhd->hgij", queries, new_keys, preferred_element_type=jnp.float32)
        * score_scale
    )
    new_scores = jnp.where(new_valid[None, None], new_scores, -jnp.inf)

    def fill_scores(block_index, buffer):
        key_piece = lax.dynamic_slice_in_dim(stored, block_index * key_block, key_block, 0)
        scores = (
            jnp.einsum(
                "ihgd,khd->hgik",
                queries,
                key_piece[..., :head_size],
                preferred_element_type=jnp.float32,
            )
            * score_scale
        )
        key_valid = block_index * key_block + jnp.arange(key_block, dtype=jnp.int32) < cached_count
        scores = jnp.where(key_valid[None, None, None, :], scores, -jnp.inf)
        return lax.dynamic_update_slice_in_dim(buffer, scores, block_index * key_block, 3)

    empty_scores = jnp.full((heads_here, group_size, row_count, slot_length), -jnp.inf, jnp.float32)
    score_buffer = lax.fori_loop(0, block_count, fill_scores, empty_scores)
    highest = jnp.maximum(jnp.max(score_buffer, axis=-1), jnp.max(new_scores, axis=-1))
    new_weights = jnp.exp(new_scores - highest[..., None])
    totals = jnp.sum(new_weights, axis=-1)
    summed = jnp.einsum(
        "hgij,jhd->ihgd",
        new_weights.astype(jnp.bfloat16),
        new_values,
        preferred_element_type=jnp.float32,
    )

    def accumulate(block_index, running_pair):
        totals_now, summed_now = running_pair
        scores = lax.dynamic_slice_in_dim(score_buffer, block_index * key_block, key_block, 3)
        value_piece = lax.dynamic_slice_in_dim(stored, block_index * key_block, key_block, 0)
        weights = jnp.exp(scores - highest[..., None])
        added = jnp.einsum(
            "hgik,khd->ihgd",
            weights.astype(jnp.bfloat16),
            value_piece[..., head_size:],
            preferred_element_type=jnp.float32,
        )
        return (totals_now + jnp.sum(weights, axis=-1), summed_now + added)

    totals, summed = lax.fori_loop(0, block_count, accumulate, (totals, summed))
    return (summed / jnp.transpose(totals, (2, 0, 1))[..., None]).astype(jnp.bfloat16)


def per_device(
    activations,
    input_gain,
    qkv_weight,
    out_weight,
    post_gain,
    cache_entries,
    new_lengths,
    cache_lengths,
    request_slot,
):
    req_count = lax.axis_size("req")
    kv_count = lax.axis_size("kv")
    token_count = activations.shape[0] * kv_count
    tok_blk = token_count // req_count
    query_rows = tok_blk * 3 // 4
    width_slice = activations.shape[1]
    width_all = width_slice * req_count
    kvh_local = qkv_weight.shape[1]
    head_size = cache_entries.shape[3] // 2
    group_size = qkv_weight.shape[2] // head_size - 2
    per_block = cache_entries.shape[0]
    slot_length = cache_entries.shape[1]
    key_block = min(512, slot_length)
    token_of_row, row_of_token, pos_of_row, pos_of_token, slot_of_row, offset_row = layout(
        new_lengths, cache_lengths, request_slot, tok_blk
    )
    inputs_f32 = activations.astype(jnp.float32)
    square_total = lax.psum(jnp.sum(inputs_f32 * inputs_f32, axis=1), "req")
    normed_in = (
        inputs_f32
        * lax.rsqrt(square_total / width_all + epsilon_norm)[:, None]
        * input_gain.astype(jnp.float32)[None, :]
    ).astype(jnp.bfloat16)
    rows_all = lax.all_gather(normed_in, "kv", axis=0, tiled=True)
    weight_flat = qkv_weight.reshape(width_slice, -1)
    block_id = lax.axis_index("req")
    first_row = block_id * tok_blk
    qkv_sums = lax.psum_scatter(
        jnp.dot(rows_all, weight_flat, preferred_element_type=jnp.float32),
        "req",
        scatter_dimension=0,
        tiled=True,
    )
    my_positions = lax.dynamic_slice_in_dim(pos_of_token, first_row, tok_blk, 0)
    own_rotated = rotate(
        qkv_sums.reshape(tok_blk, kvh_local, group_size + 2, head_size),
        my_positions,
        group_size,
        head_size,
    ).astype(jnp.bfloat16)
    all_rows = lax.all_gather(own_rotated.reshape(tok_blk, -1), "req", axis=0, tiled=True)
    wanted = lax.dynamic_slice_in_dim(token_of_row, first_row, tok_blk, 0)
    rotated = jnp.take(all_rows, wanted, axis=0).reshape(
        tok_blk, kvh_local, group_size + 2, head_size
    )
    appended = rotated[:, :, group_size:, :].reshape(tok_blk, kvh_local, 2 * head_size)
    new_counts = lax.dynamic_index_in_dim(new_lengths, block_id, 0, keepdims=False)
    cached_counts = lax.dynamic_index_in_dim(cache_lengths, block_id, 0, keepdims=False)
    starts = jnp.cumsum(new_counts) - new_counts
    slot_outputs = []
    for slot_index in range(per_block):
        picked = jnp.minimum(
            starts[slot_index] + jnp.arange(query_rows, dtype=jnp.int32), tok_blk - 1
        )
        slot_rows = jnp.take(rotated, picked, axis=0)
        block_count = slot_length // key_block
        slot_outputs.append(
            slot_attention(
                slot_rows[:, :, :group_size, :],
                slot_rows[:, :, group_size, :],
                slot_rows[:, :, group_size + 1, :],
                cache_entries[slot_index],
                cached_counts[slot_index],
                new_counts[slot_index],
                block_count,
                key_block,
            )
        )
    stacked = jnp.stack(slot_outputs).reshape(per_block * query_rows, -1)
    local_slot = lax.dynamic_slice_in_dim(slot_of_row, first_row, tok_blk, 0) - block_id * per_block
    local_offset = lax.dynamic_slice_in_dim(offset_row, first_row, tok_blk, 0)
    attention = jnp.take(stacked, local_slot * query_rows + local_offset, axis=0)
    out_flat = out_weight.reshape(-1, width_slice)
    block_projection = jnp.dot(
        lax.all_gather(attention, "req", axis=0, tiled=True),
        out_flat,
        preferred_element_type=jnp.float32,
    )
    token_rows = jnp.take(block_projection, row_of_token, axis=0)
    projection = lax.psum_scatter(
        token_rows.astype(jnp.bfloat16), "kv", scatter_dimension=0, tiled=True
    ).astype(jnp.float32)
    projected = projection.astype(jnp.bfloat16)
    residual = inputs_f32 + projection
    residual_total = lax.psum(jnp.sum(residual * residual, axis=1), "req")
    normed = (
        residual
        * lax.rsqrt(residual_total / width_all + epsilon_norm)[:, None]
        * post_gain.astype(jnp.float32)[None, :]
    ).astype(jnp.bfloat16)
    return (projected, normed, appended)


def solution(mesh):
    in_specs = (
        P("kv", "req"),
        P("req"),
        P("req", "kv", None),
        P("kv", None, "req"),
        P("req"),
        P("req", None, "kv", None),
        P(),
        P(),
        P(),
    )
    out_specs = (P("kv", "req"), P("kv", "req"), P("req", "kv", None))
    return jax.shard_map(
        per_device, mesh=mesh, in_specs=in_specs, out_specs=out_specs, check_vma=False
    )
```

profile of v0, /device:TPU:0, one launch (start us, length us, event | category | flops | bytes accessed | tf_op | source)
XLA Modules:
  0.0 1020.1 jit_solution(11127864479354095447)
XLA Ops:
  9.1 23.1 %psum.14 = f32[256]{0:T(256)S(1)} all-reduce(f32[256]{0:T(256)S(1)} %fusion.75), channel_id=1, replica_groups=mesh['req'=8,'kv'=4] {'req'}, use_global_device_ids=true, to_apply=%region_12.13 | all-reduce | flops 256 | bytes 2048 | tf_op jit(solution)/shard_map/psum | solution.py:155
  34.3 5.8 copy.96
  40.1 14.2 %all-gather.4.cloned.1.call-done = bf16[1024,1024]{1,0:T(8,128)(2,1)} async-done(((bf16[256,1024]{1,0:T(8,128)(2,1)}), bf16[1024,1024]{1,0:T(8,128)(2,1)}) %all-gather.4.cloned.1.call-update) | async-done | bytes 2097168 | tf_op jit(solution)/shard_map/all_gather | solution.py:161
  54.3 10.9 %fusion.119 = f32[1024,2560]{1,0:T(8,128)} fusion(bf16[1024,1024]{1,0:T(8,128)(2,1)} %all-gather.4.cloned.1.call-done, bf16[1024,2560]{1,0:T(8,128)(2,1)} %bitcast.302), kind=kOutput, calls=%fused_computation.242 | convolution fusion | flops 5368709120 | bytes 17825792 | tf_op jit(solution)/shard_map/dot_general | solution.py:166
  68.3 175.0 %reduce-scatter.3.cloned.1.call-done = f32[128,2560]{1,0:T(8,128)} async-done(((f32[1024,2560]{1,0:T(8,128)}), f32[128,2560]{1,0:T(8,128)}) %reduce-scatter.3.cloned.1.call-update) | async-done | bytes 1310736 | tf_op jit(solution)/shard_map/reduce_scatter | solution.py:165
  247.0 16.3 %fusion.110 = (bf16[1,4096,2,256]{3,2,1,0:T(2,128)(2,1)S(1)}, bf16[1,4096,2,256]{3,2,1,0:T(2,128)(2,1)S(1)}, bf16[1,4096,2,256]{3,2,1,0:T(2,128)(2,1)S(1)}, bf16...) fusion(bf16[5,4096,2,256]{3,2,1,0:T(2,128)(2,1)} %param.36), kind=kLoop, calls=%fused_computation.233 | loop fusion | bytes 41943040 | tf_op jit(solution)/shard_map/slice | solution.py:199
  283.3 4.2 copy_bitcast_fusion
  287.6 4.2 copy_bitcast_fusion.2
  291.8 40.2 %all-gather.6.cloned.1.call-done = bf16[1024,2560]{1,0:T(8,128)(2,1)} async-done(((bf16[128,2560]{1,0:T(8,128)(2,1)}), bf16[1024,2560]{1,0:T(8,128)(2,1)}) %all-gather.6.cloned.1.call-update) | async-done | bytes 5242896 | tf_op jit(solution)/shard_map/all_gather | solution.py:178
  332.0 4.8 gather_fusion
  340.5 11.5 %broadcast.381.clone.4 = f32[2,8,96,4096]{3,2,1,0:T(8,128)} broadcast(f32[]{:T(128)} %constant.483.clone.1), dimensions={} | broadcast | bytes 25165828 | tf_op jit(solution)/shard_map/broadcast.17
  352.0 31.0 %while.148 = (s32[]{:T(128)}, f32[2,8,96,4096]{3,2,1,0:T(8,128)}, s32[]{:T(128)}, bf16[4096,2,256]{2,0,1:T(8,128)(2,1)}, bf16[96,2,8,128]{3,0,2,1:T(8,128)(2,1)S...) while((s32[]{:T(128)}, f32[2,8,96,4096]{3,2,1,0:T(8,128)}, s32[]{:T(128)}, ...), condition=%wide.region_49.51_spmd, body=%wide.region_48.50_spmd.sunk | while | flops 202900480 | bytes 3803283 | solution.py:99
  352.7 3.2 bitcast_dynamic-update-slice_fusion.19
  356.6 3.2 bitcast_dynamic-update-slice_fusion.19
  360.6 3.2 bitcast_dynamic-update-slice_fusion.19
  372.1 3.2 bitcast_dynamic-update-slice_fusion.19
  376.0 3.2 bitcast_dynamic-update-slice_fusion.19
  383.5 9.4 reduce_max.98
  395.7 11.5 %broadcast.381.clone.3 = f32[2,8,96,4096]{3,2,1,0:T(8,128)} broadcast(f32[]{:T(128)} %constant.483.clone.1), dimensions={} | broadcast | bytes 25165828 | tf_op jit(solution)/shard_map/broadcast.17
  407.2 30.0 %while.146 = (s32[]{:T(128)}, f32[2,8,96,4096]{3,2,1,0:T(8,128)}, s32[]{:T(128)}, bf16[4096,2,256]{2,0,1:T(8,128)(2,1)}, bf16[96,2,8,128]{3,0,2,1:T(8,128)(2,1)S...) while((s32[]{:T(128)}, f32[2,8,96,4096]{3,2,1,0:T(8,128)}, s32[]{:T(128)}, ...), condition=%wide.region_41.43_spmd, body=%wide.region_40.42_spmd.sunk | while | flops 202900480 | bytes 3803283 | solution.py:99
  407.8 3.2 bitcast_dynamic-update-slice_fusion.18
  411.6 3.2 bitcast_dynamic-update-slice_fusion.18
  437.6 9.2 reduce_max.96
  450.4 11.5 %broadcast.381.clone.2 = f32[2,8,96,4096]{3,2,1,0:T(8,128)} broadcast(f32[]{:T(128)} %constant.483.clone.1), dimensions={} | broadcast | bytes 25165828 | tf_op jit(solution)/shard_map/broadcast.17
  461.9 31.1 %while.144 = (s32[]{:T(128)}, f32[2,8,96,4096]{3,2,1,0:T(8,128)}, s32[]{:T(128)}, bf16[4096,2,256]{2,0,1:T(8,128)(2,1)}, bf16[96,2,8,128]{3,0,2,1:T(8,128)(2,1)S...) while((s32[]{:T(128)}, f32[2,8,96,4096]{3,2,1,0:T(8,128)}, s32[]{:T(128)}, ...), condition=%wide.region_33.35_spmd, body=%wide.region_32.34_spmd.sunk | while | flops 202900480 | bytes 3803283 | solution.py:99
  462.5 3.4 bitcast_dynamic-update-slice_fusion.17
  466.5 3.4 bitcast_dynamic-update-slice_fusion.17
  470.5 3.2 bitcast_dynamic-update-slice_fusion.17
  474.4 3.2 bitcast_dynamic-update-slice_fusion.17
  478.2 3.2 bitcast_dynamic-update-slice_fusion.17
  482.1 3.2 bitcast_dynamic-update-slice_fusion.17
  485.9 3.2 bitcast_dynamic-update-slice_fusion.17
  489.8 3.2 bitcast_dynamic-update-slice_fusion.17
  494.3 9.4 reduce_max.94
  510.9 11.5 %broadcast.381.clone.1 = f32[2,8,96,4096]{3,2,1,0:T(8,128)} broadcast(f32[]{:T(128)} %constant.483.clone.1), dimensions={} | broadcast | bytes 25165828 | tf_op jit(solution)/shard_map/broadcast.17
  522.4 30.6 %while.142 = (s32[]{:T(128)}, f32[2,8,96,4096]{3,2,1,0:T(8,128)}, s32[]{:T(128)}, bf16[4096,2,256]{2,0,1:T(8,128)(2,1)}, bf16[96,2,8,128]{3,0,2,1:T(8,128)(2,1)S...) while((s32[]{:T(128)}, f32[2,8,96,4096]{3,2,1,0:T(8,128)}, s32[]{:T(128)}, ...), condition=%wide.region_25.27_spmd, body=%wide.region_24.26_spmd.sunk | while | flops 202900480 | bytes 3803283 | solution.py:99
  523.0 3.2 bitcast_dynamic-update-slice_fusion.16
  526.9 3.2 bitcast_dynamic-update-slice_fusion.16
  554.3 9.2 reduce_max.92
  566.9 3.7 gather_fusion.3
  572.5 11.5 %broadcast.381.clone = f32[2,8,96,4096]{3,2,1,0:T(8,128)} broadcast(f32[]{:T(128)} %constant.483.clone.1), dimensions={} | broadcast | bytes 25165828 | tf_op jit(solution)/shard_map/broadcast.17
  584.0 30.3 %while.140 = (s32[]{:T(128)}, f32[2,8,96,4096]{3,2,1,0:T(8,128)}, s32[]{:T(128)}, bf16[4096,2,256]{2,0,1:T(8,128)(2,1)}, bf16[96,2,8,128]{3,0,2,1:T(8,128)(2,1)S...) while((s32[]{:T(128)}, f32[2,8,96,4096]{3,2,1,0:T(8,128)}, s32[]{:T(128)}, ...), condition=%wide.region_17.19_spmd, body=%wide.region_16.18_spmd.sunk | while | flops 202900480 | bytes 3803283 | solution.py:99
  584.7 3.2 bitcast_dynamic-update-slice_fusion.15
  588.5 3.2 bitcast_dynamic-update-slice_fusion.15
  616.7 9.2 reduce_max.90
  629.7 44.7 %while.149 = (s32[]{:T(128)}, f32[2,8,96]{2,1,0:T(8,128)S(1)}, f32[96,2,8,128]{3,0,2,1:T(8,128)S(1)}, f32[2,8,96,4096]{3,2,1,0:T(8,128)}, f32[2,8,96]{2,1,0:T(8,...) while((s32[]{:T(128)}, f32[2,8,96]{2,1,0:T(8,128)S(1)}, ...), condition=%wide.region_55.57_spmd, body=%wide.region_53.56_spmd.sunk | while | flops 204668928 | bytes 8165035 | solution.py:123
  674.4 44.9 %while.147 = (s32[]{:T(128)}, f32[2,8,96]{2,1,0:T(8,128)S(1)}, f32[96,2,8,128]{3,0,2,1:T(8,128)S(1)}, f32[2,8,96,4096]{3,2,1,0:T(8,128)}, f32[2,8,96]{2,1,0:T(8,...) while((s32[]{:T(128)}, f32[2,8,96]{2,1,0:T(8,128)S(1)}, ...), condition=%wide.region_47.49_spmd, body=%wide.region_45.48_spmd.sunk | while | flops 204668928 | bytes 8165035 | solution.py:123
  719.4 44.7 %while.145 = (s32[]{:T(128)}, f32[2,8,96]{2,1,0:T(8,128)S(1)}, f32[96,2,8,128]{3,0,2,1:T(8,128)S(1)}, f32[2,8,96,4096]{3,2,1,0:T(8,128)}, f32[2,8,96]{2,1,0:T(8,...) while((s32[]{:T(128)}, f32[2,8,96]{2,1,0:T(8,128)S(1)}, ...), condition=%wide.region_39.41_spmd, body=%wide.region_37.40_spmd.sunk | while | flops 204668928 | bytes 8165035 | solution.py:123
  764.1 44.7 %while.143 = (s32[]{:T(128)}, f32[2,8,96]{2,1,0:T(8,128)S(1)}, f32[96,2,8,128]{3,0,2,1:T(8,128)S(1)}, f32[2,8,96,4096]{3,2,1,0:T(8,128)}, f32[2,8,96]{2,1,0:T(8,...) while((s32[]{:T(128)}, f32[2,8,96]{2,1,0:T(8,128)S(1)}, ...), condition=%wide.region_31.33_spmd, body=%wide.region_29.32_spmd.sunk | while | flops 204668928 | bytes 8165035 | solution.py:123
  808.8 51.6 %while.141 = (s32[]{:T(128)}, f32[2,8,96]{2,1,0:T(8,128)S(1)}, f32[96,2,8,128]{3,0,2,1:T(8,128)}, f32[2,8,96,4096]{3,2,1,0:T(8,128)}, f32[2,8,96]{2,1,0:T(8,128)...) while((s32[]{:T(128)}, f32[2,8,96]{2,1,0:T(8,128)S(1)}, ...), condition=%wide.region_23.25_spmd, body=%wide.region_21.24_spmd.sunk | while | flops 204668928 | bytes 8165035 | solution.py:123
  808.8 3.8 fusion.154
  815.2 3.8 fusion.154
  821.7 3.8 fusion.154
  828.1 3.8 fusion.154
  834.6 3.8 fusion.154
  841.0 3.8 fusion.154
  847.5 3.8 fusion.154
  853.9 3.8 fusion.154
  870.5 71.3 %all-gather.8.cloned.1.call-done = bf16[1024,2048]{1,0:T(8,128)(2,1)} async-done(((bf16[128,2048]{1,0:T(8,128)(2,1)}), bf16[1024,2048]{1,0:T(8,128)(2,1)}) %all-gather.8.cloned.1.call-update) | async-done | bytes 4194320 | tf_op jit(solution)/shard_map/all_gather | solution.py:212
  941.8 8.0 fusion.120
  949.7 5.4 gather_fusion.2
  955.1 3.4 select_convert_fusion
  960.2 28.2 %reduce-scatter.5.cloned.1.call-done = bf16[256,1024]{1,0:T(8,128)(2,1)} async-done(((bf16[1024,1024]{1,0:T(8,128)(2,1)}), bf16[256,1024]{1,0:T(8,128)(2,1)}) %reduce-scatter.5.cloned.1.call-update) | async-done | bytes 524304 | tf_op jit(solution)/shard_map/reduce_scatter | solution.py:217
  989.7 21.3 %psum.15 = f32[256]{0:T(256)S(1)} all-reduce(f32[256]{0:T(256)S(1)} %multiply_reduce_fusion), channel_id=1, replica_groups=mesh['req'=8,'kv'=4] {'req'}, use_global_device_ids=true, to_apply=%region_58.60 | all-reduce | flops 256 | bytes 2048 | tf_op jit(solution)/shard_map/psum | solution.py:222
  (348 shorter events, 367.6 us)
Async XLA Ops:
  7.2 47.1 %all-gather.4.cloned.1.call-start = ((), (), s32[]{:S(2)}) async-start(), calls=%async_computation.2 | async-start | bytes 2621440 | tf_op jit(solution)/shard_map/all_gather | solution.py:161
  34.3 209.0 %reduce-scatter.3.cloned.1.call-start = ((), (), s32[]{:S(2)}) async-start(), calls=%async_computation.3 | async-start | bytes 11796480 | tf_op jit(solution)/shard_map/reduce_scatter | solution.py:165
  65.2 0.7 copy-start.15
  65.2 0.9 copy-start.22
  65.2 1.6 copy-start.17
  65.3 266.7 %all-gather.6.cloned.1.call-start = ((), (), s32[]{:S(2)}) async-start(), calls=%async_computation.4 | async-start | bytes 5898240 | tf_op jit(solution)/shard_map/all_gather | solution.py:178
  67.3 0.8 copy-start.12
  246.4 695.3 %all-gather.8.cloned.1.call-start = ((), (), s32[]{:S(2)}) async-start(), calls=%async_computation.5 | async-start | bytes 4718592 | tf_op jit(solution)/shard_map/all_gather | solution.py:212
  338.8 168.3 %copy-start = (bf16[128,2,10,128]{3,1,2,0:T(2,128)(2,1)}, bf16[128,2,10,128]{3,1,2,0:T(2,128)(2,1)S(1)}, u32[]{:S(2)}) copy-start(bf16[128,2,10,128]{3,1,2,0:T(2,128)(2,1)S(1)} %broadcast_select_fusion) | copy-start | bytes 1966084
  407.2 30.0 %copy-start.14 = (pred[96,96]{0,1:T(8,128)(4,1)S(1)}, pred[96,96]{0,1:T(8,128)(4,1)}, u32[]{:S(2)}) copy-start(pred[96,96]{0,1:T(8,128)(4,1)} %fusion.99) | copy-start | bytes 27652
  503.8 5.9 copy-start.18
  503.8 18.6 %copy-start.4 = (f32[2,8,96]{2,1,0:T(8,128)}, f32[2,8,96]{2,1,0:T(8,128)S(1)}, u32[]{:S(2)}) copy-start(f32[2,8,96]{2,1,0:T(8,128)S(1)} %max.37) | copy-start | bytes 18436
  510.8 42.1 %copy-start.3 = (bf16[96,2,10,128]{3,0,2,1:T(8,128)(2,1)}, bf16[96,2,10,128]{3,0,2,1:T(8,128)(2,1)S(1)}, u32[]{:S(2)}) copy-start(bf16[96,2,10,128]{3,0,2,1:T(8,128)(2,1)S(1)} %copy_select_fusion.3) | copy-start | bytes 1474564
  563.5 7.1 copy-start.21
  563.5 7.0 copy-start.6
  571.7 0.8 copy-start.2
  616.7 13.0 %copy-start.8 = (f32[2,8,96]{2,1,0:T(8,128)S(1)}, f32[2,8,96]{2,1,0:T(8,128)}, u32[]{:S(2)}) copy-start(f32[2,8,96]{2,1,0:T(8,128)} %fusion.87) | copy-start | bytes 18436
  629.7 44.7 %copy-start.9 = (f32[2,8,96]{2,1,0:T(8,128)S(1)}, f32[2,8,96]{2,1,0:T(8,128)}, u32[]{:S(2)}) copy-start(f32[2,8,96]{2,1,0:T(8,128)} %fusion.85) | copy-start | bytes 18436
  674.4 44.9 %copy-start.5 = (f32[2,8,96]{2,1,0:T(8,128)S(1)}, f32[2,8,96]{2,1,0:T(8,128)}, u32[]{:S(2)}) copy-start(f32[2,8,96]{2,1,0:T(8,128)} %copy-done.4) | copy-start | bytes 18436
  674.4 44.9 %copy-start.10 = (f32[2,8,96]{2,1,0:T(8,128)S(1)}, f32[2,8,96]{2,1,0:T(8,128)}, u32[]{:S(2)}) copy-start(f32[2,8,96]{2,1,0:T(8,128)} %fusion.83) | copy-start | bytes 18436
  719.3 44.7 %copy-start.7 = (f32[2,8,96]{2,1,0:T(8,128)S(1)}, f32[2,8,96]{2,1,0:T(8,128)}, u32[]{:S(2)}) copy-start(f32[2,8,96]{2,1,0:T(8,128)} %copy-done.6) | copy-start | bytes 18436
  719.3 44.7 %copy-start.11 = (f32[2,8,96]{2,1,0:T(8,128)S(1)}, f32[2,8,96]{2,1,0:T(8,128)}, u32[]{:S(2)}) copy-start(f32[2,8,96]{2,1,0:T(8,128)} %fusion.81) | copy-start | bytes 18436
  868.0 1.1 copy-start.19
  868.0 2.4 copy-start.13
  868.0 2.4 copy-start.16
  870.1 118.3 %reduce-scatter.5.cloned.1.call-start = ((), (), s32[]{:S(2)}) async-start(), calls=%async_computation.6 | async-start | bytes 2621440 | tf_op jit(solution)/shard_map/reduce_scatter | solution.py:217
  955.1 3.5 copy-start.20
  955.1 33.3 %copy-start.1 = (bf16[256,1024]{1,0:T(8,128)(2,1)S(1)}, bf16[256,1024]{1,0:T(8,128)(2,1)}, u32[]{:S(2)}) copy-start(bf16[256,1024]{1,0:T(8,128)(2,1)} %param.31) | copy-start | bytes 1572868
Sparse Core Ops, SparseCore 0:
  34.4 19.8 all-gather.3
  65.4 177.8 reduce-scatter.2
  246.5 85.4 all-gather.5
  870.2 71.5 all-gather.7
  958.7 29.6 reduce-scatter.4
where the time goes:
time: 1030 us; the launch traced here: 1020 us
  waiting for transfers between devices  329 us (32%)
  matrix products  281 us (27%)
  other arithmetic  220 us (21%)
  local copies, waits for them, and re-layouts  127 us (12%)
  blocking collectives  44.4 us (4%)
  between operations  15.1 us (1%)
    reduce_scatter x1, waiting for transfers between devices, per_device(): lax.psum_scatter(jnp.dot(rows_all, weight_flat, preferred_element_type=jn...  175 us
    dot_general x40, matrix products, fill_scores(): jnp.einsum('ihgd,khd->hgik', queries, key_piece[..., :head_size], preferr...  128 us
    dot_general x40, matrix products, accumulate(): jnp.einsum('hgik,khd->ihgd', weights.astype(jnp.bfloat16), value_piece[.....  123 us
    reduce_sum x40, other arithmetic, accumulate(): return (totals_now + jnp.sum(weights, axis=-1), summed_now + added)  106 us
    all_gather x1, waiting for transfers between devices, per_device(): lax.all_gather(attention, 'req', axis=0, tiled=True)  71.3 us
    another operation x7, local copies, waits for them, and re-layouts  57.6 us
    reduce_max x5, other arithmetic, slot_attention(): jnp.max(score_buffer, axis=-1)  46.6 us
    all_gather x1, waiting for transfers between devices, per_device(): lax.all_gather(own_rotated.reshape(tok_blk, -1), 'req', axis=0, tiled=True)  40.2 us
  transfers between devices with their start and end apart: 5, of which 5 were waited for; matrix products, arithmetic and copies ran while one was open for 5% of the time, Pallas kernels for 0%

commit v1 on v0

v1 whole, which is shorter than its diff:
```python
import functools
import math

import jax
import jax.numpy as jnp
from jax import lax
from jax.experimental import pallas as pl
from jax.experimental.pallas import tpu as pltpu
from jax.sharding import PartitionSpec as P

epsilon_norm = 1e-05
rope_base = 500000.0


def layout(new_lengths, cache_lengths, request_slot, block_tokens):
    blocks, per_block = new_lengths.shape
    request_total = blocks * per_block
    token_total = blocks * block_tokens
    slot_ids = jnp.arange(request_total, dtype=jnp.int32)
    new_flat = new_lengths.reshape(request_total)
    cache_flat = cache_lengths.reshape(request_total)
    chosen = (request_slot[:, None] == slot_ids[None, :]).astype(jnp.int32)
    arrival_len = jnp.sum(chosen * new_flat[None, :], axis=1)
    arrival_start = jnp.cumsum(arrival_len) - arrival_len
    inside = jnp.cumsum(new_lengths, axis=1) - new_lengths
    slot_start = (inside + block_tokens * jnp.arange(blocks, dtype=jnp.int32)[:, None]).reshape(
        request_total
    )
    slot_arrival_start = jnp.sum(chosen * arrival_start[:, None], axis=0)
    positions = jnp.arange(token_total, dtype=jnp.int32)
    slot_of_row = jnp.sum((slot_start[None, :] <= positions[:, None]).astype(jnp.int32), axis=1) - 1
    row_pick = (slot_of_row[:, None] == slot_ids[None, :]).astype(jnp.int32)
    offset_row = positions - jnp.sum(row_pick * slot_start[None, :], axis=1)
    token_of_row = jnp.sum(row_pick * slot_arrival_start[None, :], axis=1) + offset_row
    pos_of_row = jnp.sum(row_pick * cache_flat[None, :], axis=1) + offset_row
    arrival_of_token = (
        jnp.sum((arrival_start[None, :] <= positions[:, None]).astype(jnp.int32), axis=1) - 1
    )
    token_pick = (arrival_of_token[:, None] == slot_ids[None, :]).astype(jnp.int32)
    slot_of_token = jnp.sum(token_pick * request_slot[None, :], axis=1)
    offset_token = positions - jnp.sum(token_pick * arrival_start[None, :], axis=1)
    token_slot_pick = (slot_of_token[:, None] == slot_ids[None, :]).astype(jnp.int32)
    row_of_token = jnp.sum(token_slot_pick * slot_start[None, :], axis=1) + offset_token
    pos_of_token = jnp.sum(token_slot_pick * cache_flat[None, :], axis=1) + offset_token
    return (token_of_row, row_of_token, pos_of_row, pos_of_token, slot_of_row, offset_row)


def rotate(partial_sums, positions, group_size, head_size):
    half_size = head_size // 2
    frequency = jnp.exp(
        -(jnp.arange(half_size, dtype=jnp.float32) * (2.0 / head_size)) * math.log(rope_base)
    )
    angles = positions.astype(jnp.float32)[:, None] * frequency[None, :]
    cosine = jnp.cos(angles)[:, None, None, :]
    sine_part = jnp.sin(angles)[:, None, None, :]
    turned = partial_sums[:, :, : group_size + 1, :]
    first_half = turned[..., :half_size]
    second_half = turned[..., half_size:]
    turned = jnp.concatenate(
        [
            first_half * cosine - second_half * sine_part,
            second_half * cosine + first_half * sine_part,
        ],
        axis=-1,
    )
    return jnp.concatenate([turned, partial_sums[:, :, group_size + 1 :, :]], axis=2)


def attention_kernel(
    group_size, key_block, cached_ref, new_ref, q_ref, key_ref, value_ref, stored_ref, out_ref, keys, values, scores
):
    slot = pl.program_id(0)
    cached_count = cached_ref[slot]
    new_count = new_ref[slot]
    heads, rows_all, head_size = q_ref.shape[1:]
    most_new = key_ref.shape[2]
    slot_length = stored_ref.shape[1]
    chunk = min(256, rows_all)
    chunk_tokens = chunk // group_size
    block_count = (cached_count + key_block - 1) // key_block
    scale = math.log2(math.e) / math.sqrt(head_size)

    def split_heads(index, carry):
        at = pl.ds(pl.multiple_of(index * key_block, key_block), key_block)
        for head in range(heads):
            piece = stored_ref[0, at, head, :]
            keys[head, at, :] = piece[:, :head_size]
            values[head, at, :] = piece[:, head_size:]
        return carry

    lax.fori_loop(0, block_count, split_heads, 0)

    def lane_fold(op, value):
        folded = value[:, :head_size]
        for part in range(1, value.shape[1] // head_size):
            folded = op(folded, value[:, part * head_size : (part + 1) * head_size])
        return folded

    contract_last = (((1,), (1,)), ((), ()))
    for head in range(heads):
        for part in range(rows_all // chunk):

            @pl.when(part * chunk_tokens < new_count)
            def _(head=head, part=part):
                rows = pl.ds(part * chunk, chunk)
                query = q_ref[0, head, rows, :]
                columns = lax.broadcasted_iota(jnp.int32, (chunk, most_new), 1)
                offsets = part * chunk_tokens + (
                    lax.broadcasted_iota(jnp.int32, (chunk, most_new), 0) // group_size
                )
                own = lax.dot_general(
                    query, key_ref[0, head], contract_last, preferred_element_type=jnp.float32
                )
                own = jnp.where((columns <= offsets) & (columns < new_count), own, -jnp.inf)
                places = lax.broadcasted_iota(jnp.int32, (chunk, key_block), 1)

                def fill(index, highest):
                    first = pl.multiple_of(index * key_block, key_block)
                    found = lax.dot_general(
                        query,
                        keys[head, pl.ds(first, key_block), :],
                        contract_last,
                        preferred_element_type=jnp.float32,
                    )
                    found = jnp.where(places < cached_count - first, found, -jnp.inf)
                    scores[:, pl.ds(first, key_block)] = found
                    return jnp.maximum(highest, lane_fold(jnp.maximum, found))

                highest = lax.fori_loop(
                    0, block_count, fill, jnp.full((chunk, head_size), -jnp.inf, jnp.float32)
                )
                top = jnp.maximum(
                    jnp.max(highest, axis=1, keepdims=True), jnp.max(own, axis=1, keepdims=True)
                )
                own_weights = jnp.exp2((own - top) * scale)
                summed = jnp.dot(
                    own_weights.astype(jnp.bfloat16),
                    value_ref[0, head],
                    preferred_element_type=jnp.float32,
                )

                def accumulate(index, pair):
                    first = pl.multiple_of(index * key_block, key_block)
                    weights = jnp.exp2((scores[:, pl.ds(first, key_block)] - top) * scale)
                    added = jnp.dot(
                        weights.astype(jnp.bfloat16),
                        values[head, pl.ds(first, key_block), :],
                        preferred_element_type=jnp.float32,
                    )
                    return (pair[0] + lane_fold(jnp.add, weights), pair[1] + added)

                totals, summed = lax.fori_loop(
                    0,
                    block_count,
                    accumulate,
                    (jnp.zeros((chunk, head_size), jnp.float32), summed),
                )
                total = jnp.sum(totals, axis=1, keepdims=True) + jnp.sum(
                    own_weights, axis=1, keepdims=True
                )
                out_ref[0, head, rows, :] = (summed / total).astype(out_ref.dtype)


def block_attention(queries, new_keys, new_values, stored, cached_counts, new_counts, group_size):
    slots, heads, rows, head_size = queries.shape
    most_new = new_keys.shape[2]
    slot_length = stored.shape[1]
    key_block = min(512, slot_length)
    grid_spec = pltpu.PrefetchScalarGridSpec(
        num_scalar_prefetch=2,
        grid=(slots,),
        in_specs=[
            pl.BlockSpec((1, heads, rows, head_size), lambda s, c, n: (s, 0, 0, 0)),
            pl.BlockSpec((1, heads, most_new, head_size), lambda s, c, n: (s, 0, 0, 0)),
            pl.BlockSpec((1, heads, most_new, head_size), lambda s, c, n: (s, 0, 0, 0)),
            pl.BlockSpec((1, slot_length, heads, 2 * head_size), lambda s, c, n: (s, 0, 0, 0)),
        ],
        out_specs=pl.BlockSpec((1, heads, rows, head_size), lambda s, c, n: (s, 0, 0, 0)),
        scratch_shapes=[
            pltpu.VMEM((heads, slot_length, head_size), jnp.bfloat16),
            pltpu.VMEM((heads, slot_length, head_size), jnp.bfloat16),
            pltpu.VMEM((min(256, rows), slot_length), jnp.float32),
        ],
    )
    return pl.pallas_call(
        functools.partial(attention_kernel, group_size, key_block),
        grid_spec=grid_spec,
        out_shape=jax.ShapeDtypeStruct(queries.shape, jnp.bfloat16),
        compiler_params=pltpu.CompilerParams(vmem_limit_bytes=48 << 20),
    )(cached_counts, new_counts, queries, new_keys, new_values, stored)


def per_device(
    activations,
    input_gain,
    qkv_weight,
    out_weight,
    post_gain,
    cache_entries,
    new_lengths,
    cache_lengths,
    request_slot,
):
    req_count = lax.axis_size("req")
    kv_count = lax.axis_size("kv")
    token_count = activations.shape[0] * kv_count
    tok_blk = token_count // req_count
    query_rows = tok_blk * 3 // 4
    width_slice = activations.shape[1]
    width_all = width_slice * req_count
    kvh_local = qkv_weight.shape[1]
    head_size = cache_entries.shape[3] // 2
    group_size = qkv_weight.shape[2] // head_size - 2
    per_block = cache_entries.shape[0]
    token_of_row, row_of_token, pos_of_row, pos_of_token, slot_of_row, offset_row = layout(
        new_lengths, cache_lengths, request_slot, tok_blk
    )
    inputs_f32 = activations.astype(jnp.float32)
    square_total = lax.psum(jnp.sum(inputs_f32 * inputs_f32, axis=1), "req")
    normed_in = (
        inputs_f32
        * lax.rsqrt(square_total / width_all + epsilon_norm)[:, None]
        * input_gain.astype(jnp.float32)[None, :]
    ).astype(jnp.bfloat16)
    rows_all = lax.all_gather(normed_in, "kv", axis=0, tiled=True)
    rows_all = jnp.take(rows_all, token_of_row, axis=0)
    weight_flat = qkv_weight.reshape(width_slice, -1)
    block_id = lax.axis_index("req")
    first_row = block_id * tok_blk
    qkv_sums = lax.psum_scatter(
        jnp.dot(rows_all, weight_flat, preferred_element_type=jnp.float32),
        "req",
        scatter_dimension=0,
        tiled=True,
    )
    my_positions = lax.dynamic_slice_in_dim(pos_of_row, first_row, tok_blk, 0)
    rotated = rotate(
        qkv_sums.reshape(tok_blk, kvh_local, group_size + 2, head_size),
        my_positions,
        group_size,
        head_size,
    ).astype(jnp.bfloat16)
    appended = rotated[:, :, group_size:, :].reshape(tok_blk, kvh_local, 2 * head_size)
    new_counts = lax.dynamic_index_in_dim(new_lengths, block_id, 0, keepdims=False)
    cached_counts = lax.dynamic_index_in_dim(cache_lengths, block_id, 0, keepdims=False)
    starts = jnp.cumsum(new_counts) - new_counts
    picked = jnp.minimum(
        starts[:, None] + jnp.arange(query_rows, dtype=jnp.int32)[None, :], tok_blk - 1
    ).reshape(-1)
    slot_rows = jnp.take(rotated.reshape(tok_blk, -1), picked, axis=0).reshape(
        per_block, query_rows, kvh_local, group_size + 2, head_size
    )
    queries = jnp.transpose(slot_rows[:, :, :, :group_size], (0, 2, 1, 3, 4)).reshape(
        per_block, kvh_local, query_rows * group_size, head_size
    )
    stacked = block_attention(
        queries,
        jnp.transpose(slot_rows[:, :, :, group_size], (0, 2, 1, 3)),
        jnp.transpose(slot_rows[:, :, :, group_size + 1], (0, 2, 1, 3)),
        cache_entries,
        cached_counts,
        new_counts,
        group_size,
    )
    stacked = jnp.transpose(
        stacked.reshape(per_block, kvh_local, query_rows, -1), (0, 2, 1, 3)
    ).reshape(per_block * query_rows, -1)
    local_slot = lax.dynamic_slice_in_dim(slot_of_row, first_row, tok_blk, 0) - block_id * per_block
    local_offset = lax.dynamic_slice_in_dim(offset_row, first_row, tok_blk, 0)
    attention = jnp.take(stacked, local_slot * query_rows + local_offset, axis=0)
    out_flat = out_weight.reshape(-1, width_slice)
    block_projection = jnp.dot(
        lax.all_gather(attention, "req", axis=0, tiled=True),
        out_flat,
        preferred_element_type=jnp.float32,
    )
    token_rows = jnp.take(block_projection.astype(jnp.bfloat16), row_of_token, axis=0)
    projection = lax.psum_scatter(
        token_rows, "kv", scatter_dimension=0, tiled=True
    ).astype(jnp.float32)
    projected = projection.astype(jnp.bfloat16)
    residual = inputs_f32 + projection
    residual_total = lax.psum(jnp.sum(residual * residual, axis=1), "req")
    normed = (
        residual
        * lax.rsqrt(residual_total / width_all + epsilon_norm)[:, None]
        * post_gain.astype(jnp.float32)[None, :]
    ).astype(jnp.bfloat16)
    return (projected, normed, appended)


def solution(mesh):
    in_specs = (
        P("kv", "req"),
        P("req"),
        P("req", "kv", None),
        P("kv", None, "req"),
        P("req"),
        P("req", None, "kv", None),
        P(),
        P(),
        P(),
    )
    out_specs = (P("kv", "req"), P("kv", "req"), P("req", "kv", None))
    return jax.shard_map(
        per_device, mesh=mesh, in_specs=in_specs, out_specs=out_specs, check_vma=False
    )
```

time: 1030 us -> 478 us (0.46)
  matrix products: 281 us -> 18.9 us
  other arithmetic: 220 us -> 17.5 us
  local copies, waits for them, and re-layouts: 127 us -> 38.7 us
  Pallas kernels: 0 us -> 26.7 us
  waiting for transfers between devices: 329 us -> 308 us
    dot_general x90 -> x0, matrix products: 262 us -> none  [the longest x40 128 us: fill_scores(): jnp.einsum('ihgd,khd->hgik', queries, key_piece[..., :head_size], preferr...]
    reduce_sum x47 -> x2, other arithmetic: 113 us -> 0.26 us  [the longest x1 0.16 us: layout(): pos_of_row = jnp.sum(row_pick * cache_flat[None, :], axis=1) + offset_row]
    another operation x8 -> x2, local copies, waits for them, and re-layouts: 59.6 us -> 0.1 us
    reduce_max x5 -> x0, other arithmetic: 46.6 us -> none  [slot_attention(): jnp.max(score_buffer, axis=-1)]
    all_gather x1 -> x0, waiting for transfers between devices: 40.2 us -> none  [per_device(): lax.all_gather(own_rotated.reshape(tok_blk, -1), 'req', axis=0, tiled=True)]
    lt x45 -> x0, other arithmetic: 28.3 us -> none  [the longest x40 25.2 us: fill_scores(): block_index * key_block + jnp.arange(key_block, dtype=jnp.int32)]
    pallas_call x0 -> x1, Pallas kernels: none -> 26.7 us  [block_attention(): pl.pallas_call(functools.partial(attention_kernel, group_size, key_block)...]
    all_gather x1, waiting for transfers between devices: 71.3 us -> 91.3 us  [per_device(): lax.all_gather(attention, 'req', axis=0, tiled=True)]
  transfers between devices with their start and end apart: 5 -> 4, of which waited for: 5 -> 4; matrix products, arithmetic and copies ran while one was open for 5% -> 2% of each run, Pallas kernels for 0% -> 0%
where the time goes in v1:
time: 478 us; the launch traced here: 469 us
  waiting for transfers between devices  308 us (64%)
  blocking collectives  44.4 us (9%)
  local copies, waits for them, and re-layouts  38.7 us (8%)
  Pallas kernels  26.7 us (6%)
  matrix products  18.9 us (4%)
  other arithmetic  17.5 us (4%)
  between operations  14.1 us (3%)
    reduce_scatter x1, waiting for transfers between devices, per_device(): lax.psum_scatter(jnp.dot(rows_all, weight_flat, preferred_element_type=jn...  177 us
    all_gather x1, waiting for transfers between devices, per_device(): lax.all_gather(attention, 'req', axis=0, tiled=True)  91.3 us
    reduce_scatter x1, waiting for transfers between devices, per_device(): lax.psum_scatter(token_rows, 'kv', scatter_dimension=0, tiled=True)  27.5 us
    pallas_call x1, Pallas kernels, block_attention(): pl.pallas_call(functools.partial(attention_kernel, group_size, key_block)...  26.7 us
    psum x1, blocking collectives, per_device(): square_total = lax.psum(jnp.sum(inputs_f32 * inputs_f32, axis=1), 'req')  23.1 us
    psum x1, blocking collectives, per_device(): residual_total = lax.psum(jnp.sum(residual * residual, axis=1), 'req')  21.3 us
    all_gather x1, waiting for transfers between devices, per_device(): rows_all = lax.all_gather(normed_in, 'kv', axis=0, tiled=True)  12.5 us
    dot_general x1, matrix products, per_device(): jnp.dot(rows_all, weight_flat, preferred_element_type=jnp.float32)  10.9 us
  transfers between devices with their start and end apart: 4, of which 4 were waited for; matrix products, arithmetic and copies ran while one was open for 2% of the time, Pallas kernels for 0%

profile of v1, /device:TPU:0, one launch (start us, length us, event | category | flops | bytes accessed | tf_op | source)
XLA Modules:
  0.0 468.9 jit_solution(3295102128074575035)
XLA Ops:
  7.2 0.0 all-gather.3.cloned.1.call-start
  7.2 0.7 convert_element_type.44
  7.9 1.2 fusion.3
  9.2 23.1 %psum.14 = f32[256]{0:T(256)S(1)} all-reduce(f32[256]{0:T(256)S(1)} %fusion.3), channel_id=1, replica_groups=mesh['req'=8,'kv'=4] {'req'}, use_global_device_ids=true, to_apply=%region_5.6 | all-reduce | flops 256 | bytes 2048 | tf_op jit(solution)/shard_map/psum | solution.py:219
  32.3 2.0 fusion.5
  34.3 0.0 all-gather.3.cloned.1.call-update
  34.3 0.0 reduce-scatter.3.cloned.1.call-start
  34.4 0.1 mul.199
  34.4 0.2 select_reduce_fusion.7
  34.6 0.1 copy.21
  34.7 0.2 reduce_window_sum.25
  34.9 0.1 reduce-window.16
  34.9 0.1 reduce
  35.1 0.1 subtract_add_fusion
  35.2 0.1 le.54
  35.2 0.1 mul.206
  35.3 5.9 %copy.28 = bf16[128,8,2,1280]{3,1,2,0:T(8,128)(2,1)} copy(bf16[128,8,2,1280]{3,2,1,0:T(2,128)(2,1)} %bitcast.43) | data formatting | bytes 10485760
  41.2 0.1 convert_reduce_fusion
  41.3 0.1 convert_reduce_fusion.1
  41.4 0.1 select_reduce_fusion.6
  41.5 0.1 select_reduce_fusion
  41.6 0.2 select_reduce_fusion.3
  41.8 12.5 %all-gather.3.cloned.1.call-done = bf16[1024,1024]{1,0:T(8,128)(2,1)} async-done(((bf16[256,1024]{1,0:T(8,128)(2,1)}), bf16[1024,1024]{1,0:T(8,128)(2,1)}) %all-gather.3.cloned.1.call-update) | async-done | bytes 2097168 | tf_op jit(solution)/shard_map/all_gather | solution.py:225
  54.3 6.8 %gather_fusion.2 = bf16[1024,1024]{1,0:T(8,128)(2,1)S(1)} fusion(bf16[1024,1024]{1,0:T(8,128)(2,1)} %all-gather.3.cloned.1.call-done, s32[1024]{0:T(1024)S(1)} %get-tuple-element.25), kind=kCustom, calls=%fused_computation.clone | custom fusion | bytes 4198400 | tf_op jit(solution)/shard_map/jit(_take)/gather | solution.py:226
  61.2 10.9 %fusion = f32[1024,2560]{1,0:T(8,128)} fusion(bf16[1024,2560]{1,0:T(8,128)(2,1)} %bitcast.44, bf16[1024,1024]{1,0:T(8,128)(2,1)S(1)} %gather_fusion.2, pred[1024]{0:T(1024)(128)(4,1)S(1)} %compare_and_fusion.1), kind=kOutput, calls=%fused_computation.5 | convolution fusion | flops 5369757696 | bytes 17826816 | tf_op jit(solution)/shard_map/dot_general | solution.py:231
  72.1 0.0 reduce-scatter.3.cloned.1.call-update
  72.1 0.2 all-gather.5.cloned.1.call-start
  72.4 0.2 reduce-window.15
  72.6 0.1 add_minimum_fusion
  72.7 0.1 min.22
  72.8 0.1 dynamic-slice_convert_fusion
  72.8 0.1 compare_and_fusion.3
  73.0 0.1 compare_and_fusion.2
  73.0 0.2 multiply_cosine_fusion
  73.2 177.0 %reduce-scatter.3.cloned.1.call-done = f32[128,2560]{1,0:T(8,128)} async-done(((f32[1024,2560]{1,0:T(8,128)}), f32[128,2560]{1,0:T(8,128)}) %reduce-scatter.3.cloned.1.call-update) | async-done | bytes 1310736 | tf_op jit(solution)/shard_map/reduce_scatter | solution.py:230
  250.2 1.7 copy.22
  251.9 0.2 multiply_subtract_fusion
  252.2 0.8 copy-done.1
  253.0 0.3 copy.23
  253.3 2.6 gather_fusion
  255.9 3.6 gather.14
  259.5 4.0 copy_select_fusion
  263.5 0.1 slice_bitcast_fusion
  263.7 1.3 copy.32
  265.0 26.7 %shard_map.112 = bf16[5,2,768,128]{3,2,1,0:T(8,128)(2,1)S(1)} custom-call(s32[5]{0:T(128)S(1)} %dynamic-slice_bitcast_fusion.cached_ref, s32[5]{0:T(128)S(1)} %get-tuple-element.19.new_ref, bf16[5,2,768,128]{3,2,1,0:T(8,128)(2,1)S(1)} %bitcast.39, bf16[5,2,96,128]{3,2,1,0:T(8,128)(2,1)S(1)} %get-tuple-element.21.key_ref, ...), custom_call_target="tpu_custom_call" | custom-call | tf_op jit(solution)/shard_map/pallas_call | solution.py:185
  291.6 2.3 reshape.227
  293.9 3.6 copy.26
  297.5 0.5 copy.29
  298.0 0.9 gather_fusion.1
  299.0 0.9 broadcast_select_fusion.1
  299.9 0.0 all-gather.5.cloned.1.call-update
  299.9 0.0 reduce-scatter.5.cloned.1.call-start
  300.0 91.3 %all-gather.5.cloned.1.call-done = bf16[1024,2048]{1,0:T(8,128)(2,1)} async-done(((bf16[128,2048]{1,0:T(8,128)(2,1)}), bf16[1024,2048]{1,0:T(8,128)(2,1)}) %all-gather.5.cloned.1.call-update) | async-done | bytes 4194320 | tf_op jit(solution)/shard_map/all_gather | solution.py:273
  391.3 7.9 %convolution_convert_fusion = bf16[1024,1024]{1,0:T(8,128)(2,1)S(1)} fusion(bf16[1024,2048]{1,0:T(8,128)(2,1)} %all-gather.5.cloned.1.call-done, bf16[2048,1024]{1,0:T(8,128)(2,1)} %bitcast.51), kind=kOutput, calls=%fused_computation.11 | convolution fusion | flops 4296015872 | bytes 10485760 | tf_op jit(solution)/shard_map/dot_general | solution.py:272
  399.3 5.4 %gather_fusion.3 = bf16[1024,1024]{1,0:T(8,128)(2,1)} fusion(bf16[1024,1024]{1,0:T(8,128)(2,1)S(1)} %convolution_convert_fusion, s32[1024]{0:T(1024)S(1)} %broadcast_clamp_fusion), kind=kCustom, calls=%fused_computation.1.clone | custom fusion | bytes 4198400 | tf_op jit(solution)/shard_map/jit(_take)/gather | solution.py:277
  404.6 3.2 broadcast_select_fusion
  407.8 0.0 reduce-scatter.5.cloned.1.call-update
  407.9 0.7 copy-done.4
  408.5 0.9 slice.45
  409.4 0.8 copy.27
  410.2 27.5 %reduce-scatter.5.cloned.1.call-done = bf16[256,1024]{1,0:T(8,128)(2,1)} async-done(((bf16[1024,1024]{1,0:T(8,128)(2,1)}), bf16[256,1024]{1,0:T(8,128)(2,1)}) %reduce-scatter.5.cloned.1.call-update) | async-done | bytes 524304 | tf_op jit(solution)/shard_map/reduce_scatter | solution.py:278
  437.7 1.3 multiply_reduce_fusion
  439.0 21.3 %psum.15 = f32[256]{0:T(256)S(1)} all-reduce(f32[256]{0:T(256)S(1)} %multiply_reduce_fusion), channel_id=1, replica_groups=mesh['req'=8,'kv'=4] {'req'}, use_global_device_ids=true, to_apply=%region_18.20 | all-reduce | flops 256 | bytes 2048 | tf_op jit(solution)/shard_map/psum | solution.py:283
  460.4 2.0 multiply_convert_fusion
  (31 shorter events, 0.2 us)
Async XLA Ops:
  7.2 27.2 %copy-start.2 = (s32[8,5]{1,0:T(8,128)S(1)}, s32[8,5]{1,0:T(8,128)}, u32[]{:S(2)}) copy-start(s32[8,5]{1,0:T(8,128)} %param.17) | copy-start | bytes 484
  7.2 27.3 %copy-start.5 = (s32[40]{0:T(128)S(1)}, s32[40]{0:T(128)}, u32[]{:S(2)}) copy-start(s32[40]{0:T(128)} %param.19) | copy-start | bytes 484
  7.2 28.1 %copy-start.3 = (s32[8,5]{1,0:T(8,128)S(1)}, s32[8,5]{1,0:T(8,128)}, u32[]{:S(2)}) copy-start(s32[8,5]{1,0:T(8,128)} %param.18) | copy-start | bytes 484
  7.2 47.2 %all-gather.3.cloned.1.call-start = ((), (), s32[]{:S(2)}) async-start(), calls=%async_computation.2 | async-start | bytes 2621440 | tf_op jit(solution)/shard_map/all_gather | solution.py:225
  34.3 215.9 %reduce-scatter.3.cloned.1.call-start = ((), (), s32[]{:S(2)}) async-start(), calls=%async_computation.3 | async-start | bytes 11796480 | tf_op jit(solution)/shard_map/reduce_scatter | solution.py:230
  72.1 319.2 %all-gather.5.cloned.1.call-start = ((), (), s32[]{:S(2)}) async-start(), calls=%async_computation.4 | async-start | bytes 4718592 | tf_op jit(solution)/shard_map/all_gather | solution.py:273
  252.2 0.8 copy-start.1
  299.9 137.8 %reduce-scatter.5.cloned.1.call-start = ((), (), s32[]{:S(2)}) async-start(), calls=%async_computation.5 | async-start | bytes 2621440 | tf_op jit(solution)/shard_map/reduce_scatter | solution.py:278
  407.8 0.7 copy-start.4
  407.8 29.9 %copy-start = (bf16[256,1024]{1,0:T(8,128)(2,1)S(1)}, bf16[256,1024]{1,0:T(8,128)(2,1)}, u32[]{:S(2)}) copy-start(bf16[256,1024]{1,0:T(8,128)(2,1)} %param.11) | copy-start | bytes 1572868
Sparse Core Ops, SparseCore 0:
  34.4 19.8 all-gather.2
  72.3 177.8 reduce-scatter.2
  300.0 91.2 all-gather.4
  408.0 29.7 reduce-scatter.4

commit v2 on v1

--- a/solution.py
+++ b/solution.py
@@ -3,6 +3,7 @@
 
 import jax
 import jax.numpy as jnp
+import numpy as np
 from jax import lax
 from jax.experimental import pallas as pl
 from jax.experimental.pallas import tpu as pltpu
@@ -188,6 +189,84 @@
         out_shape=jax.ShapeDtypeStruct(queries.shape, jnp.bfloat16),
         compiler_params=pltpu.CompilerParams(vmem_limit_bytes=48 << 20),
     )(cached_counts, new_counts, queries, new_keys, new_values, stored)
+
+
+def ring_table(count):
+    across = 1
+    while 4 * across * across <= count:
+        across *= 2
+    along = count // across
+    ring = [place * across for place in range(along)]
+    for turn, place in enumerate(reversed(range(along))):
+        row = [place * across + step for step in range(1, across)]
+        ring += row if turn % 2 == 0 else row[::-1]
+    order = np.zeros((count, count), np.int32)
+    slot_of = np.zeros((count, count), np.int32)
+    for start in range(count):
+        for step in range(count):
+            order[ring[start], step] = ring[(start + step) % count]
+            slot_of[ring[start], ring[(start + step) % count]] = step
+    ahead = [(ring[i], ring[(i + 1) % count]) for i in range(count)]
+    return order, slot_of, ahead, [(b, a) for a, b in ahead]
+
+
+def ring_project_scatter(rows, weight, count, ahead, behind):
+    block = rows.shape[0] // count
+    columns = weight.shape[1]
+    parts = 2
+    width = columns // parts
+    made = {}
+
+    def product(index):
+        if index not in made:
+            made[index] = jnp.dot(
+                rows[index * block : (index + 1) * block],
+                weight,
+                preferred_element_type=jnp.float32,
+            )
+        return made[index]
+
+    def piece(index, part):
+        return product(index % count)[:, part * width : (part + 1) * width]
+
+    forward = [part % 2 == 0 for part in range(parts)]
+    held = [piece(-1 if forward[part] else 1, part) for part in range(parts)]
+    for step in range(count - 1):
+        moved = [
+            lax.ppermute(held[part], "req", ahead if forward[part] else behind)
+            for part in range(parts)
+        ]
+        held = [
+            moved[part] + piece(-2 - step if forward[part] else 2 + step, part)
+            for part in range(parts)
+        ]
+    return jnp.concatenate(held, axis=1)
+
+
+def ring_gather_project(own, weight, count, ahead, behind):
+    results = [None] * count
+    results[0] = jnp.dot(own, weight, preferred_element_type=jnp.float32).astype(jnp.bfloat16)
+    half = own.shape[1] // 2
+    from_behind = from_ahead = own
+    for step in range(1, (count + 1) // 2):
+        from_behind = lax.ppermute(from_behind, "req", ahead)
+        from_ahead = lax.ppermute(from_ahead, "req", behind)
+        for index, arrived in ((count - step, from_behind), (step, from_ahead)):
+            results[index] = jnp.dot(
+                arrived, weight, preferred_element_type=jnp.float32
+            ).astype(jnp.bfloat16)
+    if count % 2 == 0:
+        last = jnp.concatenate(
+            [
+                lax.ppermute(from_behind[:, :half], "req", ahead),
+                lax.ppermute(from_ahead[:, half:], "req", behind),
+            ],
+            axis=1,
+        )
+        results[count // 2] = jnp.dot(
+            last, weight, preferred_element_type=jnp.float32
+        ).astype(jnp.bfloat16)
+    return jnp.concatenate(results, axis=0)
 
 
 def per_device(
@@ -223,16 +302,20 @@
         * input_gain.astype(jnp.float32)[None, :]
     ).astype(jnp.bfloat16)
     rows_all = lax.all_gather(normed_in, "kv", axis=0, tiled=True)
-    rows_all = jnp.take(rows_all, token_of_row, axis=0)
-    weight_flat = qkv_weight.reshape(width_slice, -1)
     block_id = lax.axis_index("req")
     first_row = block_id * tok_blk
-    qkv_sums = lax.psum_scatter(
-        jnp.dot(rows_all, weight_flat, preferred_element_type=jnp.float32),
-        "req",
-        scatter_dimension=0,
-        tiled=True,
-    )
+    order, slot_of, ahead, behind = ring_table(req_count)
+    ring_order = lax.dynamic_index_in_dim(jnp.asarray(order), block_id, 0, keepdims=False)
+    ring_slot = lax.dynamic_index_in_dim(jnp.asarray(slot_of), block_id, 0, keepdims=False)
+    ring_pick = (
+        ring_order[:, None] == jnp.arange(req_count, dtype=jnp.int32)[None, :]
+    ).astype(jnp.int32)
+    ring_rows = jnp.sum(
+        ring_pick[:, :, None] * token_of_row.reshape(req_count, tok_blk)[None], axis=1
+    ).reshape(-1)
+    rows_all = jnp.take(rows_all, ring_rows, axis=0, mode="clip")
+    weight_flat = qkv_weight.reshape(width_slice, -1)
+    qkv_sums = ring_project_scatter(rows_all, weight_flat, req_count, ahead, behind)
     my_positions = lax.dynamic_slice_in_dim(pos_of_row, first_row, tok_blk, 0)
     rotated = rotate(
         qkv_sums.reshape(tok_blk, kvh_local, group_size + 2, head_size),
@@ -247,7 +330,7 @@
     picked = jnp.minimum(
         starts[:, None] + jnp.arange(query_rows, dtype=jnp.int32)[None, :], tok_blk - 1
     ).reshape(-1)
-    slot_rows = jnp.take(rotated.reshape(tok_blk, -1), picked, axis=0).reshape(
+    slot_rows = jnp.take(rotated.reshape(tok_blk, -1), picked, axis=0, mode="clip").reshape(
         per_block, query_rows, kvh_local, group_size + 2, head_size
     )
     queries = jnp.transpose(slot_rows[:, :, :, :group_size], (0, 2, 1, 3, 4)).reshape(
@@ -267,14 +350,15 @@
     ).reshape(per_block * query_rows, -1)
     local_slot = lax.dynamic_slice_in_dim(slot_of_row, first_row, tok_blk, 0) - block_id * per_block
     local_offset = lax.dynamic_slice_in_dim(offset_row, first_row, tok_blk, 0)
-    attention = jnp.take(stacked, local_slot * query_rows + local_offset, axis=0)
+    attention = jnp.take(stacked, local_slot * query_rows + local_offset, axis=0, mode="clip")
     out_flat = out_weight.reshape(-1, width_slice)
-    block_projection = jnp.dot(
-        lax.all_gather(attention, "req", axis=0, tiled=True),
-        out_flat,
-        preferred_element_type=jnp.float32,
-    )
-    token_rows = jnp.take(block_projection.astype(jnp.bfloat16), row_of_token, axis=0)
+    block_projection = ring_gather_project(attention, out_flat, req_count, ahead, behind)
+    block_of_token = row_of_token // tok_blk
+    token_pick = (
+        block_of_token[:, None] == jnp.arange(req_count, dtype=jnp.int32)[None, :]
+    ).astype(jnp.int32)
+    ring_row = jnp.sum(token_pick * ring_slot[None, :], axis=1) * tok_blk + row_of_token % tok_blk
+    token_rows = jnp.take(block_projection, ring_row, axis=0, mode="clip")
     projection = lax.psum_scatter(
         token_rows, "kv", scatter_dimension=0, tiled=True
     ).astype(jnp.float32)

time: 478 us -> 486 us (1.017); the launches traced: 469 us -> 491 us
  waiting for transfers between devices: 308 us -> 229 us
  Pallas kernels: 26.7 us -> 97 us
  starting transfers between devices: 0.35 us -> 28.6 us
    ppermute x0 -> x22, waiting for transfers between devices: none -> 192 us  [the longest x14 163 us: ring_project_scatter(): lax.ppermute(held[part], 'req', ahead if forward[part] else behind)]
    reduce_scatter x1 -> x0, waiting for transfers between devices: 177 us -> none  [per_device(): lax.psum_scatter(jnp.dot(rows_all, weight_flat, preferred_element_type=jn...]
    all_gather x1 -> x0, waiting for transfers between devices: 91.3 us -> none  [per_device(): lax.all_gather(attention, 'req', axis=0, tiled=True)]
    pallas_call x1, Pallas kernels: 26.7 us -> 97 us  [block_attention(): pl.pallas_call(functools.partial(attention_kernel, group_size, key_block)...]
    ppermute x0 -> x22, starting transfers between devices: none -> 28.5 us  [the longest x14 20.3 us: ring_project_scatter(): lax.ppermute(held[part], 'req', ahead if forward[part] else behind)]
    select_n x4 -> x0, other arithmetic: 8.12 us -> none  [the longest x2 4.01 us: per_device(): jnp.take(rotated.reshape(tok_blk, -1), picked, axis=0)]
    add x0 -> x16, other arithmetic: none -> 6.42 us  [the longest x13 6.31 us: ring_project_scatter(): moved[part] + piece(-2 - step if forward[part] else 2 + step, part)]
    reshape x0 -> x2, local copies, waits for them, and re-layouts: none -> 5.47 us  [the longest x1 3.57 us: per_device(): jnp.take(rotated.reshape(tok_blk, -1), picked, axis=0, mode='clip')]
  transfers between devices with their start and end apart: 4 -> 24, of which waited for: 4 -> 21; matrix products, arithmetic and copies ran while one was open for 2% -> 5% of each run, Pallas kernels for 0% -> 0%
where the time goes in v2:
time: 486 us; the launch traced here: 491 us
  waiting for transfers between devices  229 us (47%)
  Pallas kernels  97 us (20%)
  blocking collectives  44.4 us (9%)
  local copies, waits for them, and re-layouts  41.8 us (9%)
  starting transfers between devices  28.6 us (6%)
  matrix products  20.2 us (4%)
  other arithmetic  16 us (3%)
  between operations  14.6 us (3%)
    ppermute x14, waiting for transfers between devices, ring_project_scatter(): lax.ppermute(held[part], 'req', ahead if forward[part] else behind)  163 us
    pallas_call x1, Pallas kernels, block_attention(): pl.pallas_call(functools.partial(attention_kernel, group_size, key_block)...  97 us
    reduce_scatter x1, waiting for transfers between devices, per_device(): lax.psum_scatter(token_rows, 'kv', scatter_dimension=0, tiled=True)  25.3 us
    psum x1, blocking collectives, per_device(): square_total = lax.psum(jnp.sum(inputs_f32 * inputs_f32, axis=1), 'req')  23.1 us
    psum x1, blocking collectives, per_device(): residual_total = lax.psum(jnp.sum(residual * residual, axis=1), 'req')  21.3 us
    ppermute x14, starting transfers between devices, ring_project_scatter(): lax.ppermute(held[part], 'req', ahead if forward[part] else behind)  20.3 us
    ppermute x3, waiting for transfers between devices, ring_gather_project(): from_ahead = lax.ppermute(from_ahead, 'req', behind)  15.5 us
    dot_general x8, matrix products, product(): jnp.dot(rows[index * block:(index + 1) * block], weight, preferred_elemen...  12 us
  transfers between devices with their start and end apart: 24, of which 21 were waited for; matrix products, arithmetic and copies ran while one was open for 5% of the time, Pallas kernels for 0%

profile of v2, /device:TPU:0, one launch (start us, length us, event | category | flops | bytes accessed | tf_op | source)
XLA Modules:
  0.0 491.2 jit_solution(14461189394771787967)
XLA Ops:
  7.9 1.2 fusion.8
  9.2 23.1 %psum.14 = f32[256]{0:T(256)S(1)} all-reduce(f32[256]{0:T(256)S(1)} %fusion.8), channel_id=1, replica_groups=mesh['req'=8,'kv'=4] {'req'}, use_global_device_ids=true, to_apply=%region_1.0 | all-reduce | flops 256 | bytes 2048 | tf_op jit(solution)/shard_map/psum | solution.py:298
  32.3 2.0 fusion.10
  35.3 5.8 %copy.34 = bf16[128,8,2,1280]{3,1,2,0:T(8,128)(2,1)} copy(bf16[128,8,2,1280]{3,2,1,0:T(2,128)(2,1)} %bitcast.97) | data formatting | bytes 10485760
  42.6 11.7 %all-gather.2.cloned.1.call-done = bf16[1024,1024]{1,0:T(8,128)(2,1)} async-done(((bf16[256,1024]{1,0:T(8,128)(2,1)}), bf16[1024,1024]{1,0:T(8,128)(2,1)}) %all-gather.2.cloned.1.call-update) | async-done | bytes 2097168 | tf_op jit(solution)/shard_map/all_gather | solution.py:304
  54.4 6.8 %gather_fusion = bf16[1024,1024]{1,0:T(8,128)(2,1)S(1)} fusion(bf16[1024,1024]{1,0:T(8,128)(2,1)} %all-gather.2.cloned.1.call-done, s32[1024]{0:T(1024)S(1)} %bitcast_clamp_fusion), kind=kCustom, calls=%fused_computation | custom fusion | bytes 4198400 | tf_op jit(solution)/shard_map/jit(_take)/gather | solution.py:316
  61.2 3.5 fusion.28
  64.8 1.5 collective-permute-start
  67.2 14.5 %collective-permute-done = f32[128,1280]{1,0:T(8,128)S(1)} collective-permute-done((f32[128,1280]{1,0:T(8,128)S(1)}, f32[128,1280]{1,0:T(8,128)S(1)}, u32[]{:S(2)}, u32[]{:S(2)}) %collective-permute-start) | collective-permute-done | bytes 655392 | tf_op jit(solution)/shard_map/ppermute | solution.py:236
  81.8 1.5 collective-permute-start.1
  83.3 0.9 fusion.24
  84.2 13.7 %collective-permute-done.1 = f32[128,1280]{1,0:T(8,128)S(1)} collective-permute-done((f32[128,1280]{1,0:T(8,128)S(1)}, f32[128,1280]{1,0:T(8,128)S(1)}, u32[]{:S(2)}, u32[]{:S(2)}) %collective-permute-start.1) | collective-permute-done | bytes 655392 | tf_op jit(solution)/shard_map/ppermute | solution.py:236
  97.9 1.5 collective-permute-start.2
  100.4 12.8 %collective-permute-done.2 = f32[128,1280]{1,0:T(8,128)S(1)} collective-permute-done((f32[128,1280]{1,0:T(8,128)S(1)}, f32[128,1280]{1,0:T(8,128)S(1)}, u32[]{:S(2)}, u32[]{:S(2)}) %collective-permute-start.2) | collective-permute-done | bytes 655392 | tf_op jit(solution)/shard_map/ppermute | solution.py:236
  113.2 1.5 collective-permute-start.3
  115.6 12.4 %collective-permute-done.3 = f32[128,1280]{1,0:T(8,128)S(1)} collective-permute-done((f32[128,1280]{1,0:T(8,128)S(1)}, f32[128,1280]{1,0:T(8,128)S(1)}, u32[]{:S(2)}, u32[]{:S(2)}) %collective-permute-start.3) | collective-permute-done | bytes 655392 | tf_op jit(solution)/shard_map/ppermute | solution.py:236
  128.1 1.5 collective-permute-start.4
  130.5 12.4 %collective-permute-done.4 = f32[128,1280]{1,0:T(8,128)S(1)} collective-permute-done((f32[128,1280]{1,0:T(8,128)S(1)}, f32[128,1280]{1,0:T(8,128)S(1)}, u32[]{:S(2)}, u32[]{:S(2)}) %collective-permute-start.4) | collective-permute-done | bytes 655392 | tf_op jit(solution)/shard_map/ppermute | solution.py:236
  143.0 1.5 collective-permute-start.5
  145.4 10.2 %collective-permute-done.5 = f32[128,1280]{1,0:T(8,128)S(1)} collective-permute-done((f32[128,1280]{1,0:T(8,128)S(1)}, f32[128,1280]{1,0:T(8,128)S(1)}, u32[]{:S(2)}, u32[]{:S(2)}) %collective-permute-start.5) | collective-permute-done | bytes 655392 | tf_op jit(solution)/shard_map/ppermute | solution.py:236
  155.6 1.0 slice_add_fusion.8
  156.6 1.5 collective-permute-start.7
  158.0 13.3 %collective-permute-done.7 = f32[128,1280]{1,0:T(8,128)S(1)} collective-permute-done((f32[128,1280]{1,0:T(8,128)S(1)}, f32[128,1280]{1,0:T(8,128)S(1)}, u32[]{:S(2)}, u32[]{:S(2)}) %collective-permute-start.7) | collective-permute-done | bytes 655392 | tf_op jit(solution)/shard_map/ppermute | solution.py:236
  171.4 1.5 collective-permute-start.8
  172.9 13.3 %collective-permute-done.8 = f32[128,1280]{1,0:T(8,128)S(1)} collective-permute-done((f32[128,1280]{1,0:T(8,128)S(1)}, f32[128,1280]{1,0:T(8,128)S(1)}, u32[]{:S(2)}, u32[]{:S(2)}) %collective-permute-start.8) | collective-permute-done | bytes 655392 | tf_op jit(solution)/shard_map/ppermute | solution.py:236
  186.3 1.5 collective-permute-start.9
  187.8 13.2 %collective-permute-done.9 = f32[128,1280]{1,0:T(8,128)S(1)} collective-permute-done((f32[128,1280]{1,0:T(8,128)S(1)}, f32[128,1280]{1,0:T(8,128)S(1)}, u32[]{:S(2)}, u32[]{:S(2)}) %collective-permute-start.9) | collective-permute-done | bytes 655392 | tf_op jit(solution)/shard_map/ppermute | solution.py:236
  201.0 1.0 slice_add_fusion.4
  202.0 1.5 collective-permute-start.10
  203.4 13.2 %collective-permute-done.10 = f32[128,1280]{1,0:T(8,128)} collective-permute-done((f32[128,1280]{1,0:T(8,128)}, f32[128,1280]{1,0:T(8,128)}, u32[]{:S(2)}, u32[]{:S(2)}) %collective-permute-start.10) | collective-permute-done | bytes 655392 | tf_op jit(solution)/shard_map/ppermute | solution.py:236
  216.7 2.2 slice_add_fusion.3
  218.9 1.5 collective-permute-start.11
  220.7 15.0 %collective-permute-done.11 = f32[128,1280]{1,0:T(8,128)} collective-permute-done((f32[128,1280]{1,0:T(8,128)}, f32[128,1280]{1,0:T(8,128)}, u32[]{:S(2)}, u32[]{:S(2)}) %collective-permute-start.11) | collective-permute-done | bytes 655392 | tf_op jit(solution)/shard_map/ppermute | solution.py:236
  235.7 1.4 slice_add_fusion.2
  237.1 1.5 collective-permute-start.12
  239.3 14.0 %collective-permute-done.12 = f32[128,1280]{1,0:T(8,128)S(1)} collective-permute-done((f32[128,1280]{1,0:T(8,128)S(1)}, f32[128,1280]{1,0:T(8,128)S(1)}, u32[]{:S(2)}, u32[]{:S(2)}) %collective-permute-start.12) | collective-permute-done | bytes 655392 | tf_op jit(solution)/shard_map/ppermute | solution.py:236
  253.4 1.5 collective-permute-start.13
  255.2 3.3 fusion.14
  258.6 5.5 %collective-permute-done.13 = f32[128,1280]{1,0:T(8,128)S(1)} collective-permute-done((f32[128,1280]{1,0:T(8,128)S(1)}, f32[128,1280]{1,0:T(8,128)S(1)}, u32[]{:S(2)}, u32[]{:S(2)}) %collective-permute-start.13) | collective-permute-done | bytes 655392 | tf_op jit(solution)/shard_map/ppermute | solution.py:236
  266.1 2.8 gather_fusion.1
  268.9 3.6 reshape.328
  272.5 1.9 copy_bitcast_fusion.q_ref
  274.4 3.0 fusion.44
  277.5 97.0 %shard_map.130 = bf16[5,2,768,128]{3,2,1,0:T(8,128)(2,1)S(1)} custom-call(s32[5]{0:T(128)S(1)} %fusion.36.cached_ref, s32[5]{0:T(128)S(1)} %get-tuple-element.16.new_ref, bf16[5,2,768,128]{3,2,1,0:T(8,128)(2,1)S(1)} %copy_bitcast_fusion.q_ref, bf16[5,2,96,128]{3,2,1,0:T(8,128)(2,1)S(1)} %bitcast.77, bf16[5,2,96,128]{3,2,1,0:T(8,128)(2,1)S(1)} %bitcast.76, ...), custom_call_target="tpu_custom_call" | custom-call | tf_op jit(solution)/shard_map/pallas_call | solution.py:186
  374.5 2.3 reshape.330
  376.8 3.6 copy.30
  380.9 0.9 gather_fusion.2
  381.9 2.0 collective-permute-start.17
  384.0 9.9 %collective-permute-done.14 = bf16[128,2048]{1,0:T(8,128)(2,1)S(1)} collective-permute-done((bf16[128,2048]{1,0:T(8,128)(2,1)S(1)}, bf16[128,2048]{1,0:T(8,128)(2,1)S(1)}, u32[]{:S(2)}, u32[]{:S(2)}) %collective-permute-start.14) | collective-permute-done | bytes 524320 | tf_op jit(solution)/shard_map/ppermute | solution.py:253
  394.0 2.0 collective-permute-start.18
  396.0 3.0 fusion.7
  399.1 5.6 %collective-permute-done.15 = bf16[128,2048]{1,0:T(8,128)(2,1)S(1)} collective-permute-done((bf16[128,2048]{1,0:T(8,128)(2,1)S(1)}, bf16[128,2048]{1,0:T(8,128)(2,1)S(1)}, u32[]{:S(2)}, u32[]{:S(2)}) %collective-permute-start.15) | collective-permute-done | bytes 524320 | tf_op jit(solution)/shard_map/ppermute | solution.py:253
  404.7 1.3 collective-permute-done.18
  406.0 2.0 collective-permute-start.19
  409.5 5.7 %collective-permute-done.19 = bf16[128,2048]{1,0:T(8,128)(2,1)S(1)} collective-permute-done((bf16[128,2048]{1,0:T(8,128)(2,1)S(1)}, bf16[128,2048]{1,0:T(8,128)(2,1)S(1)}, u32[]{:S(2)}, u32[]{:S(2)}) %collective-permute-start.19) | collective-permute-done | bytes 524320 | tf_op jit(solution)/shard_map/ppermute | solution.py:252
  415.2 2.1 collective-permute-start.20
  418.1 3.5 collective-permute-done.20
  421.6 2.1 collective-permute-done.21
  426.6 5.4 %gather_fusion.3 = bf16[1024,1024]{1,0:T(8,128)(2,1)} fusion(bf16[1024,1024]{1,0:T(8,128)(2,1)S(1)} %fusion, s32[1024]{0:T(1024)S(1)} %broadcast_clamp_fusion), kind=kCustom, calls=%fused_computation.3 | custom fusion | bytes 4198400 | tf_op jit(solution)/shard_map/jit(_take)/gather | solution.py:361
  432.7 0.9 slice.175
  434.4 25.3 %reduce-scatter.2.cloned.1.call-done = bf16[256,1024]{1,0:T(8,128)(2,1)} async-done(((bf16[1024,1024]{1,0:T(8,128)(2,1)}), bf16[256,1024]{1,0:T(8,128)(2,1)}) %reduce-scatter.2.cloned.1.call-update) | async-done | bytes 524304 | tf_op jit(solution)/shard_map/reduce_scatter | solution.py:362
  459.7 1.3 multiply_reduce_fusion
  461.0 21.3 %psum.15 = f32[256]{0:T(256)S(1)} all-reduce(f32[256]{0:T(256)S(1)} %multiply_reduce_fusion), channel_id=1, replica_groups=mesh['req'=8,'kv'=4] {'req'}, use_global_device_ids=true, to_apply=%region_19.20 | all-reduce | flops 256 | bytes 2048 | tf_op jit(solution)/shard_map/psum | solution.py:367
  482.3 2.0 multiply_convert_fusion
  (110 shorter events, 19.0 us)
Async XLA Ops:
  7.2 27.2 %copy-start.6 = (s32[8,5]{1,0:T(8,128)S(1)}, s32[8,5]{1,0:T(8,128)}, u32[]{:S(2)}) copy-start(s32[8,5]{1,0:T(8,128)} %param.17) | copy-start | bytes 484
  7.2 27.3 %copy-start.9 = (s32[40]{0:T(128)S(1)}, s32[40]{0:T(128)}, u32[]{:S(2)}) copy-start(s32[40]{0:T(128)} %param.19) | copy-start | bytes 484
  7.2 28.1 %copy-start.7 = (s32[8,5]{1,0:T(8,128)S(1)}, s32[8,5]{1,0:T(8,128)}, u32[]{:S(2)}) copy-start(s32[8,5]{1,0:T(8,128)} %param.18) | copy-start | bytes 484
  7.2 47.2 %all-gather.2.cloned.1.call-start = ((), (), s32[]{:S(2)}) async-start(), calls=%async_computation.1 | async-start | bytes 2621440 | tf_op jit(solution)/shard_map/all_gather | solution.py:304
  34.3 425.4 %reduce-scatter.2.cloned.1.call-start = ((), (), s32[]{:S(2)}) async-start(), calls=%async_computation.2 | async-start | bytes 2621440 | tf_op jit(solution)/shard_map/reduce_scatter | solution.py:362
  61.2 5.1 %copy-start = (bf16[128,8,2,1280]{3,1,2,0:T(8,128)(2,1)S(1)}, bf16[128,8,2,1280]{3,1,2,0:T(8,128)(2,1)}, u32[]{:S(2)}) copy-start(bf16[128,8,2,1280]{3,1,2,0:T(8,128)(2,1)} %copy.34) | copy-start | bytes 15728644
  64.8 16.9 %collective-permute-start = (f32[128,1280]{1,0:T(8,128)S(1)}, f32[128,1280]{1,0:T(8,128)S(1)}, u32[]{:S(2)}, u32[]{:S(2)}) collective-permute-start(f32[128,1280]{1,0:T(8,128)S(1)} %slice.144), channel_id=1, source_target_pairs={{0,8},{8,16},{16,24},{24,28},{28,20},{20,12},{12,4},{4,0},{1,9},{9... | collective-permute-start | bytes 1966088 | tf_op jit(solution)/shard_map/ppermute | solution.py:236
  67.2 17.0 %copy-start.3 = (f32[128,2560]{1,0:T(8,128)}, f32[128,2560]{1,0:T(8,128)S(1)}, u32[]{:S(2)}) copy-start(f32[128,2560]{1,0:T(8,128)S(1)} %fusion.26) | copy-start | bytes 3932164
  81.8 16.1 %collective-permute-start.1 = (f32[128,1280]{1,0:T(8,128)S(1)}, f32[128,1280]{1,0:T(8,128)S(1)}, u32[]{:S(2)}, u32[]{:S(2)}) collective-permute-start(f32[128,1280]{1,0:T(8,128)S(1)} %slice_add_fusion.13), channel_id=1, source_target_pairs={{0,8},{8,16},{16,24},{24,28},{28,20},{20,12},{12,4},{4,0},{1,9},{9... | collective-permute-start | bytes 1966088 | tf_op jit(solution)/shard_map/ppermute | solution.py:236
  84.2 16.2 %copy-start.4 = (f32[128,2560]{1,0:T(8,128)}, f32[128,2560]{1,0:T(8,128)S(1)}, u32[]{:S(2)}) copy-start(f32[128,2560]{1,0:T(8,128)S(1)} %fusion.24) | copy-start | bytes 3932164
  97.9 15.2 %collective-permute-start.2 = (f32[128,1280]{1,0:T(8,128)S(1)}, f32[128,1280]{1,0:T(8,128)S(1)}, u32[]{:S(2)}, u32[]{:S(2)}) collective-permute-start(f32[128,1280]{1,0:T(8,128)S(1)} %slice_add_fusion.12), channel_id=1, source_target_pairs={{0,8},{8,16},{16,24},{24,28},{28,20},{20,12},{12,4},{4,0},{1,9},{9... | collective-permute-start | bytes 1966088 | tf_op jit(solution)/shard_map/ppermute | solution.py:236
  113.2 14.8 %collective-permute-start.3 = (f32[128,1280]{1,0:T(8,128)S(1)}, f32[128,1280]{1,0:T(8,128)S(1)}, u32[]{:S(2)}, u32[]{:S(2)}) collective-permute-start(f32[128,1280]{1,0:T(8,128)S(1)} %slice_add_fusion.11), channel_id=1, source_target_pairs={{0,8},{8,16},{16,24},{24,28},{28,20},{20,12},{12,4},{4,0},{1,9},{9... | collective-permute-start | bytes 1966088 | tf_op jit(solution)/shard_map/ppermute | solution.py:236
  128.1 14.8 %collective-permute-start.4 = (f32[128,1280]{1,0:T(8,128)S(1)}, f32[128,1280]{1,0:T(8,128)S(1)}, u32[]{:S(2)}, u32[]{:S(2)}) collective-permute-start(f32[128,1280]{1,0:T(8,128)S(1)} %slice_add_fusion.10), channel_id=1, source_target_pairs={{0,8},{8,16},{16,24},{24,28},{28,20},{20,12},{12,4},{4,0},{1,9},{9... | collective-permute-start | bytes 1966088 | tf_op jit(solution)/shard_map/ppermute | solution.py:236
  143.0 12.6 %collective-permute-start.5 = (f32[128,1280]{1,0:T(8,128)S(1)}, f32[128,1280]{1,0:T(8,128)S(1)}, u32[]{:S(2)}, u32[]{:S(2)}) collective-permute-start(f32[128,1280]{1,0:T(8,128)S(1)} %slice_add_fusion.9), channel_id=1, source_target_pairs={{0,8},{8,16},{16,24},{24,28},{28,20},{20,12},{12,4},{4,0},{1,9},{9... | collective-permute-start | bytes 1966088 | tf_op jit(solution)/shard_map/ppermute | solution.py:236
  156.6 14.7 %collective-permute-start.7 = (f32[128,1280]{1,0:T(8,128)S(1)}, f32[128,1280]{1,0:T(8,128)S(1)}, u32[]{:S(2)}, u32[]{:S(2)}) collective-permute-start(f32[128,1280]{1,0:T(8,128)S(1)} %get-tuple-element.24), channel_id=1, source_target_pairs={{8,0},{16,8},{24,16},{28,24},{20,28},{12,20},{4,12},{0,4},{9,1},{1... | collective-permute-start | bytes 1966088 | tf_op jit(solution)/shard_map/ppermute | solution.py:236
  171.4 14.8 %collective-permute-start.8 = (f32[128,1280]{1,0:T(8,128)S(1)}, f32[128,1280]{1,0:T(8,128)S(1)}, u32[]{:S(2)}, u32[]{:S(2)}) collective-permute-start(f32[128,1280]{1,0:T(8,128)S(1)} %slice_add_fusion.6), channel_id=1, source_target_pairs={{8,0},{16,8},{24,16},{28,24},{20,28},{12,20},{4,12},{0,4},{9,1},{1... | collective-permute-start | bytes 1966088 | tf_op jit(solution)/shard_map/ppermute | solution.py:236
  186.3 14.7 %collective-permute-start.9 = (f32[128,1280]{1,0:T(8,128)S(1)}, f32[128,1280]{1,0:T(8,128)S(1)}, u32[]{:S(2)}, u32[]{:S(2)}) collective-permute-start(f32[128,1280]{1,0:T(8,128)S(1)} %slice_add_fusion.5), channel_id=1, source_target_pairs={{8,0},{16,8},{24,16},{28,24},{20,28},{12,20},{4,12},{0,4},{9,1},{1... | collective-permute-start | bytes 1966088 | tf_op jit(solution)/shard_map/ppermute | solution.py:236
  202.0 14.7 %collective-permute-start.10 = (f32[128,1280]{1,0:T(8,128)}, f32[128,1280]{1,0:T(8,128)}, u32[]{:S(2)}, u32[]{:S(2)}) collective-permute-start(f32[128,1280]{1,0:T(8,128)} %slice_add_fusion.4), channel_id=1, source_target_pairs={{8,0},{16,8},{24,16},{28,24},{20,28},{12,20},{4,12},{0,4},{9,1},{1... | collective-permute-start | bytes 1966088 | tf_op jit(solution)/shard_map/ppermute | solution.py:236
  218.9 16.9 %collective-permute-start.11 = (f32[128,1280]{1,0:T(8,128)}, f32[128,1280]{1,0:T(8,128)}, u32[]{:S(2)}, u32[]{:S(2)}) collective-permute-start(f32[128,1280]{1,0:T(8,128)} %slice_add_fusion.3), channel_id=1, source_target_pairs={{8,0},{16,8},{24,16},{28,24},{20,28},{12,20},{4,12},{0,4},{9,1},{1... | collective-permute-start | bytes 1966088 | tf_op jit(solution)/shard_map/ppermute | solution.py:236
  237.1 16.2 %collective-permute-start.12 = (f32[128,1280]{1,0:T(8,128)S(1)}, f32[128,1280]{1,0:T(8,128)S(1)}, u32[]{:S(2)}, u32[]{:S(2)}) collective-permute-start(f32[128,1280]{1,0:T(8,128)S(1)} %slice_add_fusion.2), channel_id=1, source_target_pairs={{8,0},{16,8},{24,16},{28,24},{20,28},{12,20},{4,12},{0,4},{9,1},{1... | collective-permute-start | bytes 1966088 | tf_op jit(solution)/shard_map/ppermute | solution.py:236
  238.8 19.8 %collective-permute-start.6 = (f32[128,1280]{1,0:T(8,128)}, f32[128,1280]{1,0:T(8,128)S(1)}, u32[]{:S(2)}, u32[]{:S(2)}) collective-permute-start(f32[128,1280]{1,0:T(8,128)} %get-tuple-element.23), channel_id=1, source_target_pairs={{0,8},{8,16},{16,24},{24,28},{28,20},{20,12},{12,4},{4,0},{1,9},{9... | collective-permute-start | bytes 1966088 | tf_op jit(solution)/shard_map/ppermute | solution.py:236
  253.4 10.6 %collective-permute-start.13 = (f32[128,1280]{1,0:T(8,128)S(1)}, f32[128,1280]{1,0:T(8,128)S(1)}, u32[]{:S(2)}, u32[]{:S(2)}) collective-permute-start(f32[128,1280]{1,0:T(8,128)S(1)} %slice_add_fusion.1), channel_id=1, source_target_pairs={{8,0},{16,8},{24,16},{28,24},{20,28},{12,20},{4,12},{0,4},{9,1},{1... | collective-permute-start | bytes 1966088 | tf_op jit(solution)/shard_map/ppermute | solution.py:236
  265.0 0.8 copy-start.5
  381.8 12.1 %collective-permute-start.14 = (bf16[128,2048]{1,0:T(8,128)(2,1)S(1)}, bf16[128,2048]{1,0:T(8,128)(2,1)S(1)}, u32[]{:S(2)}, u32[]{:S(2)}) collective-permute-start(bf16[128,2048]{1,0:T(8,128)(2,1)S(1)} %gather_fusion.2), channel_id=1, source_target_pairs={{8,0},{16,8},{24,16},{28,24},{20,28},{12,20},{4,12},{0,4},{9,1},{1... | collective-permute-start | bytes 1572872 | tf_op jit(solution)/shard_map/ppermute | solution.py:253
  381.9 12.1 %collective-permute-start.17 = (bf16[128,2048]{1,0:T(8,128)(2,1)S(1)}, bf16[128,2048]{1,0:T(8,128)(2,1)S(1)}, u32[]{:S(2)}, u32[]{:S(2)}) collective-permute-start(bf16[128,2048]{1,0:T(8,128)(2,1)S(1)} %gather_fusion.2), channel_id=1, source_target_pairs={{0,8},{8,16},{16,24},{24,28},{28,20},{20,12},{12,4},{4,0},{1,9},{9... | collective-permute-start | bytes 1572872 | tf_op jit(solution)/shard_map/ppermute | solution.py:252
  394.0 10.7 %collective-permute-start.15 = (bf16[128,2048]{1,0:T(8,128)(2,1)S(1)}, bf16[128,2048]{1,0:T(8,128)(2,1)S(1)}, u32[]{:S(2)}, u32[]{:S(2)}) collective-permute-start(bf16[128,2048]{1,0:T(8,128)(2,1)S(1)} %collective-permute-done.14), channel_id=1, source_target_pairs={{8,0},{16,8},{24,16},{28,24},{20,28},{12,20},{4,12},{0,4},{9,1},{1... | collective-permute-start | bytes 1572872 | tf_op jit(solution)/shard_map/ppermute | solution.py:253
  394.0 12.0 %collective-permute-start.18 = (bf16[128,2048]{1,0:T(8,128)(2,1)S(1)}, bf16[128,2048]{1,0:T(8,128)(2,1)S(1)}, u32[]{:S(2)}, u32[]{:S(2)}) collective-permute-start(bf16[128,2048]{1,0:T(8,128)(2,1)S(1)} %collective-permute-done.17), channel_id=1, source_target_pairs={{0,8},{8,16},{16,24},{24,28},{28,20},{20,12},{12,4},{4,0},{1,9},{9... | collective-permute-start | bytes 1572872 | tf_op jit(solution)/shard_map/ppermute | solution.py:252
  396.0 12.0 %copy-start.1 = (bf16[2,1024,1024]{2,1,0:T(8,128)(2,1)S(1)}, bf16[2,1024,1024]{2,1,0:T(8,128)(2,1)}, u32[]{:S(2)}) copy-start(bf16[2,1024,1024]{2,1,0:T(8,128)(2,1)} %param.14) | copy-start | bytes 12582916
  404.7 12.6 %collective-permute-start.16 = (bf16[128,2048]{1,0:T(8,128)(2,1)S(1)}, bf16[128,2048]{1,0:T(8,128)(2,1)S(1)}, u32[]{:S(2)}, u32[]{:S(2)}) collective-permute-start(bf16[128,2048]{1,0:T(8,128)(2,1)S(1)} %collective-permute-done.15), channel_id=1, source_target_pairs={{8,0},{16,8},{24,16},{28,24},{20,28},{12,20},{4,12},{0,4},{9,1},{1... | collective-permute-start | bytes 1572872 | tf_op jit(solution)/shard_map/ppermute | solution.py:253
  406.0 9.2 %collective-permute-start.19 = (bf16[128,2048]{1,0:T(8,128)(2,1)S(1)}, bf16[128,2048]{1,0:T(8,128)(2,1)S(1)}, u32[]{:S(2)}, u32[]{:S(2)}) collective-permute-start(bf16[128,2048]{1,0:T(8,128)(2,1)S(1)} %collective-permute-done.18), channel_id=1, source_target_pairs={{0,8},{8,16},{16,24},{24,28},{28,20},{20,12},{12,4},{4,0},{1,9},{9... | collective-permute-start | bytes 1572872 | tf_op jit(solution)/shard_map/ppermute | solution.py:252
  415.2 6.4 %collective-permute-start.20 = (bf16[128,1024]{1,0:T(8,128)(2,1)S(1)}, bf16[128,1024]{1,0:T(8,128)(2,1)S(1)}, u32[]{:S(2)}, u32[]{:S(2)}) collective-permute-start(bf16[128,1024]{1,0:T(8,128)(2,1)S(1)} %slice.173), channel_id=1, source_target_pairs={{0,8},{8,16},{16,24},{24,28},{28,20},{20,12},{12,4},{4,0},{1,9},{9... | collective-permute-start | bytes 786440 | tf_op jit(solution)/shard_map/ppermute | solution.py:261
  417.3 6.4 %collective-permute-start.21 = (bf16[128,1024]{1,0:T(8,128)(2,1)S(1)}, bf16[128,1024]{1,0:T(8,128)(2,1)S(1)}, u32[]{:S(2)}, u32[]{:S(2)}) collective-permute-start(bf16[128,1024]{1,0:T(8,128)(2,1)S(1)} %slice.174), channel_id=1, source_target_pairs={{8,0},{16,8},{24,16},{28,24},{20,28},{12,20},{4,12},{0,4},{9,1},{1... | collective-permute-start | bytes 786440 | tf_op jit(solution)/shard_map/ppermute | solution.py:262
  432.0 0.7 copy-start.8
  432.0 27.7 %copy-start.2 = (bf16[256,1024]{1,0:T(8,128)(2,1)S(1)}, bf16[256,1024]{1,0:T(8,128)(2,1)}, u32[]{:S(2)}) copy-start(bf16[256,1024]{1,0:T(8,128)(2,1)} %param.11) | copy-start | bytes 1572868
Sparse Core Ops, SparseCore 0:
  34.4 19.8 all-gather.1
  432.1 27.5 reduce-scatter.1

commit v3 on v2

--- a/solution.py
+++ b/solution.py
@@ -232,6 +232,7 @@
     forward = [part % 2 == 0 for part in range(parts)]
     held = [piece(-1 if forward[part] else 1, part) for part in range(parts)]
     for step in range(count - 1):
+        held = lax.optimization_barrier(held)
         moved = [
             lax.ppermute(held[part], "req", ahead if forward[part] else behind)
             for part in range(parts)

time: 486 us -> 394 us (0.81); the launches traced: 491 us -> 394 us
  waiting for transfers between devices: 229 us -> 151 us
  Pallas kernels: 97 us -> 45.5 us
  starting transfers between devices: 28.6 us -> 60 us
    ppermute x14, waiting for transfers between devices: 163 us -> 81.9 us  [ring_project_scatter(): lax.ppermute(held[part], 'req', ahead if forward[part] else behind)]
    pallas_call x1, Pallas kernels: 97 us -> 45.5 us  [block_attention(): pl.pallas_call(functools.partial(attention_kernel, group_size, key_block)...]
    ppermute x3, starting transfers between devices: 6.05 us -> 39.8 us  [ring_gather_project(): from_behind = lax.ppermute(from_behind, 'req', ahead)]
    ppermute x14, starting transfers between devices: 20.3 us -> 14.6 us  [ring_project_scatter(): lax.ppermute(held[part], 'req', ahead if forward[part] else behind)]
  transfers between devices with their start and end apart: 24 -> 24, of which waited for: 21 -> 20; matrix products, arithmetic and copies ran while one was open for 5% -> 7% of each run, Pallas kernels for 0% -> 0%
where the time goes in v3:
time: 394 us
  waiting for transfers between devices  151 us (38%)
  starting transfers between devices  60 us (15%)
  Pallas kernels  45.5 us (12%)
  blocking collectives  44.5 us (11%)
  local copies, waits for them, and re-layouts  42.4 us (11%)
  matrix products  20.2 us (5%)
  other arithmetic  15.1 us (4%)
  between operations  14.6 us (4%)
    ppermute x14, waiting for transfers between devices, ring_project_scatter(): lax.ppermute(held[part], 'req', ahead if forward[part] else behind)  81.9 us
    pallas_call x1, Pallas kernels, block_attention(): pl.pallas_call(functools.partial(attention_kernel, group_size, key_block)...  45.5 us
    ppermute x3, starting transfers between devices, ring_gather_project(): from_behind = lax.ppermute(from_behind, 'req', ahead)  39.8 us
    reduce_scatter x1, waiting for transfers between devices, per_device(): lax.psum_scatter(token_rows, 'kv', scatter_dimension=0, tiled=True)  29.1 us
    psum x1, blocking collectives, per_device(): square_total = lax.psum(jnp.sum(inputs_f32 * inputs_f32, axis=1), 'req')  23.1 us
    psum x1, blocking collectives, per_device(): residual_total = lax.psum(jnp.sum(residual * residual, axis=1), 'req')  21.4 us
    ppermute x3, waiting for transfers between devices, ring_gather_project(): from_ahead = lax.ppermute(from_ahead, 'req', behind)  17.9 us
    ppermute x14, starting transfers between devices, ring_project_scatter(): lax.ppermute(held[part], 'req', ahead if forward[part] else behind)  14.6 us
  transfers between devices with their start and end apart: 24, of which 20 were waited for; matrix products, arithmetic and copies ran while one was open for 7% of the time, Pallas kernels for 0%

profile of v3, /device:TPU:0, one launch (start us, length us, event | category | flops | bytes accessed | tf_op | source)
XLA Modules:
  0.0 393.6 jit_solution(2712808526815748868)
XLA Ops:
  7.9 1.2 fusion.8
  9.2 23.1 %psum.14 = f32[256]{0:T(256)S(1)} all-reduce(f32[256]{0:T(256)S(1)} %fusion.8), channel_id=1, replica_groups=mesh['req'=8,'kv'=4] {'req'}, use_global_device_ids=true, to_apply=%region_1.0 | all-reduce | flops 256 | bytes 2048 | tf_op jit(solution)/shard_map/psum | solution.py:299
  32.3 2.0 fusion.10
  35.3 5.8 %copy.34 = bf16[128,8,2,1280]{3,1,2,0:T(8,128)(2,1)} copy(bf16[128,8,2,1280]{3,2,1,0:T(2,128)(2,1)} %bitcast.97) | data formatting | bytes 10485760
  42.6 11.7 %all-gather.2.cloned.1.call-done = bf16[1024,1024]{1,0:T(8,128)(2,1)} async-done(((bf16[256,1024]{1,0:T(8,128)(2,1)}), bf16[1024,1024]{1,0:T(8,128)(2,1)}) %all-gather.2.cloned.1.call-update) | async-done | bytes 2097168 | tf_op jit(solution)/shard_map/all_gather | solution.py:305
  54.4 6.8 %gather_fusion = bf16[1024,1024]{1,0:T(8,128)(2,1)S(1)} fusion(bf16[1024,1024]{1,0:T(8,128)(2,1)} %all-gather.2.cloned.1.call-done, s32[1024]{0:T(1024)S(1)} %bitcast_clamp_fusion), kind=kCustom, calls=%fused_computation | custom fusion | bytes 4198400 | tf_op jit(solution)/shard_map/jit(_take)/gather | solution.py:317
  61.2 3.5 fusion.26
  65.2 0.9 fusion.28
  66.2 1.5 collective-permute-start.1
  68.3 0.9 fusion.22
  69.2 0.9 fusion.24
  70.1 13.1 %collective-permute-done.1 = f32[128,1280]{1,0:T(8,128)S(1)} collective-permute-done((f32[128,1280]{1,0:T(8,128)S(1)}, f32[128,1280]{1,0:T(8,128)S(1)}, u32[]{:S(2)}, u32[]{:S(2)}) %collective-permute-start.1) | collective-permute-done | bytes 655392 | tf_op jit(solution)/shard_map/ppermute | solution.py:237
  83.2 1.1 collective-permute-done
  84.4 1.5 collective-permute-start.3
  86.0 0.9 fusion.18
  87.4 0.9 fusion.20
  88.3 11.9 %collective-permute-done.3 = f32[128,1280]{1,0:T(8,128)S(1)} collective-permute-done((f32[128,1280]{1,0:T(8,128)S(1)}, f32[128,1280]{1,0:T(8,128)S(1)}, u32[]{:S(2)}, u32[]{:S(2)}) %collective-permute-start.3) | collective-permute-done | bytes 655392 | tf_op jit(solution)/shard_map/ppermute | solution.py:237
  100.3 2.1 collective-permute-done.2
  103.0 1.5 collective-permute-start.5
  104.5 0.9 fusion.16
  105.4 11.6 %collective-permute-done.4 = f32[128,1280]{1,0:T(8,128)S(1)} collective-permute-done((f32[128,1280]{1,0:T(8,128)S(1)}, f32[128,1280]{1,0:T(8,128)S(1)}, u32[]{:S(2)}, u32[]{:S(2)}) %collective-permute-start.4) | collective-permute-done | bytes 655392 | tf_op jit(solution)/shard_map/ppermute | solution.py:237
  117.8 1.5 collective-permute-start.7
  119.9 11.4 %collective-permute-done.7 = f32[128,1280]{1,0:T(8,128)S(1)} collective-permute-done((f32[128,1280]{1,0:T(8,128)S(1)}, f32[128,1280]{1,0:T(8,128)S(1)}, u32[]{:S(2)}, u32[]{:S(2)}) %collective-permute-start.7) | collective-permute-done | bytes 655392 | tf_op jit(solution)/shard_map/ppermute | solution.py:237
  131.3 1.0 slice_add_fusion.6
  132.3 1.0 slice_add_fusion.7
  133.2 1.5 collective-permute-start.9
  135.7 10.4 %collective-permute-done.9 = f32[128,1280]{1,0:T(8,128)} collective-permute-done((f32[128,1280]{1,0:T(8,128)}, f32[128,1280]{1,0:T(8,128)}, u32[]{:S(2)}, u32[]{:S(2)}) %collective-permute-start.9) | collective-permute-done | bytes 655392 | tf_op jit(solution)/shard_map/ppermute | solution.py:237
  146.1 1.4 slice_add_fusion.4
  147.5 1.4 slice_add_fusion.5
  148.9 1.5 collective-permute-start.11
  151.1 11.3 %collective-permute-done.11 = f32[128,1280]{1,0:T(8,128)S(1)} collective-permute-done((f32[128,1280]{1,0:T(8,128)S(1)}, f32[128,1280]{1,0:T(8,128)S(1)}, u32[]{:S(2)}, u32[]{:S(2)}) %collective-permute-start.11) | collective-permute-done | bytes 655392 | tf_op jit(solution)/shard_map/ppermute | solution.py:237
  162.5 2.8 collective-permute-done.10
  165.9 1.5 collective-permute-start.13
  167.7 3.3 fusion.14
  171.0 4.9 %collective-permute-done.12 = f32[128,1280]{1,0:T(8,128)S(1)} collective-permute-done((f32[128,1280]{1,0:T(8,128)S(1)}, f32[128,1280]{1,0:T(8,128)S(1)}, u32[]{:S(2)}, u32[]{:S(2)}) %collective-permute-start.12) | collective-permute-done | bytes 655392 | tf_op jit(solution)/shard_map/ppermute | solution.py:237
  177.5 0.8 copy-done.7
  178.5 2.8 gather_fusion.1
  181.4 3.6 reshape.328
  184.9 1.9 copy_bitcast_fusion.q_ref
  186.9 3.0 fusion.44
  190.0 45.5 %shard_map.130 = bf16[5,2,768,128]{3,2,1,0:T(8,128)(2,1)S(1)} custom-call(s32[5]{0:T(128)S(1)} %fusion.36.cached_ref, s32[5]{0:T(128)S(1)} %get-tuple-element.44.new_ref, bf16[5,2,768,128]{3,2,1,0:T(8,128)(2,1)S(1)} %copy_bitcast_fusion.q_ref, bf16[5,2,96,128]{3,2,1,0:T(8,128)(2,1)S(1)} %bitcast.77, bf16[5,2,96,128]{3,2,1,0:T(8,128)(2,1)S(1)} %bitcast.76, ...), custom_call_target="tpu_custom_call" | custom-call | tf_op jit(solution)/shard_map/pallas_call | solution.py:186
  235.5 2.3 reshape.330
  237.7 3.6 copy.30
  241.9 0.9 gather_fusion.2
  242.9 2.0 collective-permute-start.17
  245.0 11.8 %collective-permute-done.14 = bf16[128,2048]{1,0:T(8,128)(2,1)S(1)} collective-permute-done((bf16[128,2048]{1,0:T(8,128)(2,1)S(1)}, bf16[128,2048]{1,0:T(8,128)(2,1)S(1)}, u32[]{:S(2)}, u32[]{:S(2)}) %collective-permute-start.14) | collective-permute-done | bytes 524320 | tf_op jit(solution)/shard_map/ppermute | solution.py:254
  257.1 1.7 collective-permute-start.18
  258.8 3.1 fusion.7
  261.9 6.1 %collective-permute-done.15 = bf16[128,2048]{1,0:T(8,128)(2,1)S(1)} collective-permute-done((bf16[128,2048]{1,0:T(8,128)(2,1)S(1)}, bf16[128,2048]{1,0:T(8,128)(2,1)S(1)}, u32[]{:S(2)}, u32[]{:S(2)}) %collective-permute-start.15) | collective-permute-done | bytes 524320 | tf_op jit(solution)/shard_map/ppermute | solution.py:254
  268.0 2.5 collective-permute-start.16
  270.5 36.1 %collective-permute-start.19 = (bf16[128,2048]{1,0:T(8,128)(2,1)S(1)}, bf16[128,2048]{1,0:T(8,128)(2,1)S(1)}, u32[]{:S(2)}, u32[]{:S(2)}) collective-permute-start(bf16[128,2048]{1,0:T(8,128)(2,1)S(1)} %collective-permute-done.18), channel_id=1, source_target_pairs={{0,8},{8,16},{16,24},{24,28},{28,20},{20,12},{12,4},{4,0},{1,9},{9... | collective-permute-start | bytes 1572872 | tf_op jit(solution)/shard_map/ppermute | solution.py:253
  308.1 5.2 %collective-permute-done.19 = bf16[128,2048]{1,0:T(8,128)(2,1)S(1)} collective-permute-done((bf16[128,2048]{1,0:T(8,128)(2,1)S(1)}, bf16[128,2048]{1,0:T(8,128)(2,1)S(1)}, u32[]{:S(2)}, u32[]{:S(2)}) %collective-permute-start.19) | collective-permute-done | bytes 524320 | tf_op jit(solution)/shard_map/ppermute | solution.py:253
  313.3 2.5 collective-permute-start.20
  315.9 0.7 fusion.4
  316.7 3.1 collective-permute-done.20
  319.7 2.6 collective-permute-done.21
  324.5 0.7 fusion
  325.2 5.4 %gather_fusion.3 = bf16[1024,1024]{1,0:T(8,128)(2,1)} fusion(bf16[1024,1024]{1,0:T(8,128)(2,1)S(1)} %fusion, s32[1024]{0:T(1024)S(1)} %broadcast_clamp_fusion), kind=kCustom, calls=%fused_computation.3 | custom fusion | bytes 4198400 | tf_op jit(solution)/shard_map/jit(_take)/gather | solution.py:362
  331.3 0.9 slice.175
  332.2 0.8 copy.31
  333.0 29.1 %reduce-scatter.2.cloned.1.call-done = bf16[256,1024]{1,0:T(8,128)(2,1)} async-done(((bf16[1024,1024]{1,0:T(8,128)(2,1)}), bf16[256,1024]{1,0:T(8,128)(2,1)}) %reduce-scatter.2.cloned.1.call-update) | async-done | bytes 524304 | tf_op jit(solution)/shard_map/reduce_scatter | solution.py:363
  362.1 1.3 multiply_reduce_fusion
  363.4 21.4 %psum.15 = f32[256]{0:T(256)S(1)} all-reduce(f32[256]{0:T(256)S(1)} %multiply_reduce_fusion), channel_id=1, replica_groups=mesh['req'=8,'kv'=4] {'req'}, use_global_device_ids=true, to_apply=%region_19.20 | all-reduce | flops 256 | bytes 2048 | tf_op jit(solution)/shard_map/psum | solution.py:368
  384.7 2.0 multiply_convert_fusion
  (114 shorter events, 17.1 us)
Async XLA Ops:
  7.2 27.2 %copy-start.8 = (s32[8,5]{1,0:T(8,128)S(1)}, s32[8,5]{1,0:T(8,128)}, u32[]{:S(2)}) copy-start(s32[8,5]{1,0:T(8,128)} %param.17) | copy-start | bytes 484
  7.2 27.3 %copy-start.11 = (s32[40]{0:T(128)S(1)}, s32[40]{0:T(128)}, u32[]{:S(2)}) copy-start(s32[40]{0:T(128)} %param.19) | copy-start | bytes 484
  7.2 28.1 %copy-start.9 = (s32[8,5]{1,0:T(8,128)S(1)}, s32[8,5]{1,0:T(8,128)}, u32[]{:S(2)}) copy-start(s32[8,5]{1,0:T(8,128)} %param.18) | copy-start | bytes 484
  7.2 47.2 %all-gather.2.cloned.1.call-start = ((), (), s32[]{:S(2)}) async-start(), calls=%async_computation.1 | async-start | bytes 2621440 | tf_op jit(solution)/shard_map/all_gather | solution.py:305
  34.3 327.8 %reduce-scatter.2.cloned.1.call-start = ((), (), s32[]{:S(2)}) async-start(), calls=%async_computation.2 | async-start | bytes 2621440 | tf_op jit(solution)/shard_map/reduce_scatter | solution.py:363
  61.2 4.0 %copy-start = (bf16[128,8,2,1280]{3,1,2,0:T(8,128)(2,1)S(1)}, bf16[128,8,2,1280]{3,1,2,0:T(8,128)(2,1)}, u32[]{:S(2)}) copy-start(bf16[128,8,2,1280]{3,1,2,0:T(8,128)(2,1)} %copy.34) | copy-start | bytes 15728644
  66.1 3.1 copy-start.3
  66.2 16.9 %collective-permute-start.1 = (f32[128,1280]{1,0:T(8,128)S(1)}, f32[128,1280]{1,0:T(8,128)S(1)}, u32[]{:S(2)}, u32[]{:S(2)}) collective-permute-start(f32[128,1280]{1,0:T(8,128)S(1)} %slice.146), channel_id=1, source_target_pairs={{8,0},{16,8},{24,16},{28,24},{20,28},{12,20},{4,12},{0,4},{9,1},{1... | collective-permute-start | bytes 1966088 | tf_op jit(solution)/shard_map/ppermute | solution.py:237
  67.7 16.6 %collective-permute-start = (f32[128,1280]{1,0:T(8,128)S(1)}, f32[128,1280]{1,0:T(8,128)S(1)}, u32[]{:S(2)}, u32[]{:S(2)}) collective-permute-start(f32[128,1280]{1,0:T(8,128)S(1)} %slice.144), channel_id=1, source_target_pairs={{0,8},{8,16},{16,24},{24,28},{28,20},{20,12},{12,4},{4,0},{1,9},{9... | collective-permute-start | bytes 1966088 | tf_op jit(solution)/shard_map/ppermute | solution.py:237
  69.2 14.0 %copy-start.5 = (f32[128,2560]{1,0:T(8,128)}, f32[128,2560]{1,0:T(8,128)S(1)}, u32[]{:S(2)}) copy-start(f32[128,2560]{1,0:T(8,128)S(1)} %fusion.22) | copy-start | bytes 3932164
  70.1 16.8 %copy-start.6 = (f32[128,2560]{1,0:T(8,128)}, f32[128,2560]{1,0:T(8,128)S(1)}, u32[]{:S(2)}) copy-start(f32[128,2560]{1,0:T(8,128)S(1)} %fusion.24) | copy-start | bytes 3932164
  84.4 15.8 %collective-permute-start.3 = (f32[128,1280]{1,0:T(8,128)S(1)}, f32[128,1280]{1,0:T(8,128)S(1)}, u32[]{:S(2)}, u32[]{:S(2)}) collective-permute-start(f32[128,1280]{1,0:T(8,128)S(1)} %slice_add_fusion.12), channel_id=1, source_target_pairs={{8,0},{16,8},{24,16},{28,24},{20,28},{12,20},{4,12},{0,4},{9,1},{1... | collective-permute-start | bytes 1966088 | tf_op jit(solution)/shard_map/ppermute | solution.py:237
  86.8 15.5 %collective-permute-start.2 = (f32[128,1280]{1,0:T(8,128)S(1)}, f32[128,1280]{1,0:T(8,128)S(1)}, u32[]{:S(2)}, u32[]{:S(2)}) collective-permute-start(f32[128,1280]{1,0:T(8,128)S(1)} %slice_add_fusion.13), channel_id=1, source_target_pairs={{0,8},{8,16},{16,24},{24,28},{28,20},{20,12},{12,4},{4,0},{1,9},{9... | collective-permute-start | bytes 1966088 | tf_op jit(solution)/shard_map/ppermute | solution.py:237
  102.4 14.6 %collective-permute-start.4 = (f32[128,1280]{1,0:T(8,128)S(1)}, f32[128,1280]{1,0:T(8,128)S(1)}, u32[]{:S(2)}, u32[]{:S(2)}) collective-permute-start(f32[128,1280]{1,0:T(8,128)S(1)} %slice_add_fusion.11), channel_id=1, source_target_pairs={{0,8},{8,16},{16,24},{24,28},{28,20},{20,12},{12,4},{4,0},{1,9},{9... | collective-permute-start | bytes 1966088 | tf_op jit(solution)/shard_map/ppermute | solution.py:237
  103.0 14.7 %collective-permute-start.5 = (f32[128,1280]{1,0:T(8,128)S(1)}, f32[128,1280]{1,0:T(8,128)S(1)}, u32[]{:S(2)}, u32[]{:S(2)}) collective-permute-start(f32[128,1280]{1,0:T(8,128)S(1)} %slice_add_fusion.10), channel_id=1, source_target_pairs={{8,0},{16,8},{24,16},{28,24},{20,28},{12,20},{4,12},{0,4},{9,1},{1... | collective-permute-start | bytes 1966088 | tf_op jit(solution)/shard_map/ppermute | solution.py:237
  117.8 13.5 %collective-permute-start.7 = (f32[128,1280]{1,0:T(8,128)S(1)}, f32[128,1280]{1,0:T(8,128)S(1)}, u32[]{:S(2)}, u32[]{:S(2)}) collective-permute-start(f32[128,1280]{1,0:T(8,128)S(1)} %get-tuple-element.24), channel_id=1, source_target_pairs={{8,0},{16,8},{24,16},{28,24},{20,28},{12,20},{4,12},{0,4},{9,1},{1... | collective-permute-start | bytes 1966088 | tf_op jit(solution)/shard_map/ppermute | solution.py:237
  119.4 12.9 %collective-permute-start.6 = (f32[128,1280]{1,0:T(8,128)S(1)}, f32[128,1280]{1,0:T(8,128)S(1)}, u32[]{:S(2)}, u32[]{:S(2)}) collective-permute-start(f32[128,1280]{1,0:T(8,128)S(1)} %get-tuple-element.23), channel_id=1, source_target_pairs={{0,8},{8,16},{16,24},{24,28},{28,20},{20,12},{12,4},{4,0},{1,9},{9... | collective-permute-start | bytes 1966088 | tf_op jit(solution)/shard_map/ppermute | solution.py:237
  133.2 12.8 %collective-permute-start.9 = (f32[128,1280]{1,0:T(8,128)}, f32[128,1280]{1,0:T(8,128)}, u32[]{:S(2)}, u32[]{:S(2)}) collective-permute-start(f32[128,1280]{1,0:T(8,128)} %slice_add_fusion.6), channel_id=1, source_target_pairs={{8,0},{16,8},{24,16},{28,24},{20,28},{12,20},{4,12},{0,4},{9,1},{1... | collective-permute-start | bytes 1966088 | tf_op jit(solution)/shard_map/ppermute | solution.py:237
  134.9 12.6 %collective-permute-start.8 = (f32[128,1280]{1,0:T(8,128)}, f32[128,1280]{1,0:T(8,128)}, u32[]{:S(2)}, u32[]{:S(2)}) collective-permute-start(f32[128,1280]{1,0:T(8,128)} %slice_add_fusion.7), channel_id=1, source_target_pairs={{0,8},{8,16},{16,24},{24,28},{28,20},{20,12},{12,4},{4,0},{1,9},{9... | collective-permute-start | bytes 1966088 | tf_op jit(solution)/shard_map/ppermute | solution.py:237
  135.6 26.8 %copy-start.4 = (f32[128,2560]{1,0:T(8,128)S(1)}, f32[128,2560]{1,0:T(8,128)}, u32[]{:S(2)}) copy-start(f32[128,2560]{1,0:T(8,128)} %copy-done.3) | copy-start | bytes 3932164
  148.9 13.5 %collective-permute-start.11 = (f32[128,1280]{1,0:T(8,128)S(1)}, f32[128,1280]{1,0:T(8,128)S(1)}, u32[]{:S(2)}, u32[]{:S(2)}) collective-permute-start(f32[128,1280]{1,0:T(8,128)S(1)} %slice_add_fusion.4), channel_id=1, source_target_pairs={{8,0},{16,8},{24,16},{28,24},{20,28},{12,20},{4,12},{0,4},{9,1},{1... | collective-permute-start | bytes 1966088 | tf_op jit(solution)/shard_map/ppermute | solution.py:237
  150.4 14.8 %collective-permute-start.10 = (f32[128,1280]{1,0:T(8,128)S(1)}, f32[128,1280]{1,0:T(8,128)S(1)}, u32[]{:S(2)}, u32[]{:S(2)}) collective-permute-start(f32[128,1280]{1,0:T(8,128)S(1)} %slice_add_fusion.5), channel_id=1, source_target_pairs={{0,8},{8,16},{16,24},{24,28},{28,20},{20,12},{12,4},{4,0},{1,9},{9... | collective-permute-start | bytes 1966088 | tf_op jit(solution)/shard_map/ppermute | solution.py:237
  165.3 10.6 %collective-permute-start.12 = (f32[128,1280]{1,0:T(8,128)S(1)}, f32[128,1280]{1,0:T(8,128)S(1)}, u32[]{:S(2)}, u32[]{:S(2)}) collective-permute-start(f32[128,1280]{1,0:T(8,128)S(1)} %slice_add_fusion.3), channel_id=1, source_target_pairs={{0,8},{8,16},{16,24},{24,28},{28,20},{20,12},{12,4},{4,0},{1,9},{9... | collective-permute-start | bytes 1966088 | tf_op jit(solution)/shard_map/ppermute | solution.py:237
  165.9 10.6 %collective-permute-start.13 = (f32[128,1280]{1,0:T(8,128)S(1)}, f32[128,1280]{1,0:T(8,128)S(1)}, u32[]{:S(2)}, u32[]{:S(2)}) collective-permute-start(f32[128,1280]{1,0:T(8,128)S(1)} %slice_add_fusion.2), channel_id=1, source_target_pairs={{8,0},{16,8},{24,16},{28,24},{20,28},{12,20},{4,12},{0,4},{9,1},{1... | collective-permute-start | bytes 1966088 | tf_op jit(solution)/shard_map/ppermute | solution.py:237
  177.4 0.8 copy-start.7
  242.8 14.0 %collective-permute-start.14 = (bf16[128,2048]{1,0:T(8,128)(2,1)S(1)}, bf16[128,2048]{1,0:T(8,128)(2,1)S(1)}, u32[]{:S(2)}, u32[]{:S(2)}) collective-permute-start(bf16[128,2048]{1,0:T(8,128)(2,1)S(1)} %gather_fusion.2), channel_id=1, source_target_pairs={{8,0},{16,8},{24,16},{28,24},{20,28},{12,20},{4,12},{0,4},{9,1},{1... | collective-permute-start | bytes 1572872 | tf_op jit(solution)/shard_map/ppermute | solution.py:254
  242.9 14.2 %collective-permute-start.17 = (bf16[128,2048]{1,0:T(8,128)(2,1)S(1)}, bf16[128,2048]{1,0:T(8,128)(2,1)S(1)}, u32[]{:S(2)}, u32[]{:S(2)}) collective-permute-start(bf16[128,2048]{1,0:T(8,128)(2,1)S(1)} %gather_fusion.2), channel_id=1, source_target_pairs={{0,8},{8,16},{16,24},{24,28},{28,20},{20,12},{12,4},{4,0},{1,9},{9... | collective-permute-start | bytes 1572872 | tf_op jit(solution)/shard_map/ppermute | solution.py:253
  256.8 11.2 %collective-permute-start.15 = (bf16[128,2048]{1,0:T(8,128)(2,1)S(1)}, bf16[128,2048]{1,0:T(8,128)(2,1)S(1)}, u32[]{:S(2)}, u32[]{:S(2)}) collective-permute-start(bf16[128,2048]{1,0:T(8,128)(2,1)S(1)} %collective-permute-done.14), channel_id=1, source_target_pairs={{8,0},{16,8},{24,16},{28,24},{20,28},{12,20},{4,12},{0,4},{9,1},{1... | collective-permute-start | bytes 1572872 | tf_op jit(solution)/shard_map/ppermute | solution.py:254
  257.1 13.4 %collective-permute-start.18 = (bf16[128,2048]{1,0:T(8,128)(2,1)S(1)}, bf16[128,2048]{1,0:T(8,128)(2,1)S(1)}, u32[]{:S(2)}, u32[]{:S(2)}) collective-permute-start(bf16[128,2048]{1,0:T(8,128)(2,1)S(1)} %collective-permute-done.17), channel_id=1, source_target_pairs={{0,8},{8,16},{16,24},{24,28},{28,20},{20,12},{12,4},{4,0},{1,9},{9... | collective-permute-start | bytes 1572872 | tf_op jit(solution)/shard_map/ppermute | solution.py:253
  258.8 47.8 %copy-start.1 = (bf16[2,1024,1024]{2,1,0:T(8,128)(2,1)S(1)}, bf16[2,1024,1024]{2,1,0:T(8,128)(2,1)}, u32[]{:S(2)}) copy-start(bf16[2,1024,1024]{2,1,0:T(8,128)(2,1)} %param.14) | copy-start | bytes 12582916
  268.0 47.8 %collective-permute-start.16 = (bf16[128,2048]{1,0:T(8,128)(2,1)S(1)}, bf16[128,2048]{1,0:T(8,128)(2,1)S(1)}, u32[]{:S(2)}, u32[]{:S(2)}) collective-permute-start(bf16[128,2048]{1,0:T(8,128)(2,1)S(1)} %collective-permute-done.15), channel_id=1, source_target_pairs={{8,0},{16,8},{24,16},{28,24},{20,28},{12,20},{4,12},{0,4},{9,1},{1... | collective-permute-start | bytes 1572872 | tf_op jit(solution)/shard_map/ppermute | solution.py:254
  270.5 42.8 %collective-permute-start.19 = (bf16[128,2048]{1,0:T(8,128)(2,1)S(1)}, bf16[128,2048]{1,0:T(8,128)(2,1)S(1)}, u32[]{:S(2)}, u32[]{:S(2)}) collective-permute-start(bf16[128,2048]{1,0:T(8,128)(2,1)S(1)} %collective-permute-done.18), channel_id=1, source_target_pairs={{0,8},{8,16},{16,24},{24,28},{28,20},{20,12},{12,4},{4,0},{1,9},{9... | collective-permute-start | bytes 1572872 | tf_op jit(solution)/shard_map/ppermute | solution.py:253
  313.3 6.4 %collective-permute-start.20 = (bf16[128,1024]{1,0:T(8,128)(2,1)S(1)}, bf16[128,1024]{1,0:T(8,128)(2,1)S(1)}, u32[]{:S(2)}, u32[]{:S(2)}) collective-permute-start(bf16[128,1024]{1,0:T(8,128)(2,1)S(1)} %slice.173), channel_id=1, source_target_pairs={{0,8},{8,16},{16,24},{24,28},{28,20},{20,12},{12,4},{4,0},{1,9},{9... | collective-permute-start | bytes 786440 | tf_op jit(solution)/shard_map/ppermute | solution.py:262
  315.9 6.4 %collective-permute-start.21 = (bf16[128,1024]{1,0:T(8,128)(2,1)S(1)}, bf16[128,1024]{1,0:T(8,128)(2,1)S(1)}, u32[]{:S(2)}, u32[]{:S(2)}) collective-permute-start(bf16[128,1024]{1,0:T(8,128)(2,1)S(1)} %slice.174), channel_id=1, source_target_pairs={{8,0},{16,8},{24,16},{28,24},{20,28},{12,20},{4,12},{0,4},{9,1},{1... | collective-permute-start | bytes 786440 | tf_op jit(solution)/shard_map/ppermute | solution.py:263
  330.6 0.7 copy-start.10
  330.6 31.5 %copy-start.2 = (bf16[256,1024]{1,0:T(8,128)(2,1)S(1)}, bf16[256,1024]{1,0:T(8,128)(2,1)}, u32[]{:S(2)}) copy-start(bf16[256,1024]{1,0:T(8,128)(2,1)} %param.11) | copy-start | bytes 1572868
Sparse Core Ops, SparseCore 0:
  34.4 19.8 all-gather.1
  330.8 31.2 reduce-scatter.1
